TPU v7x, 32 devices: a whole 2x2x4 slice. The times are simulated.
32 devices in a mesh: depth: 2 (over core), tile: 16 (over z, y, x).
Axes of the slice: x: 2, y: 2, z: 4, core: 2. Of those that a mesh axis runs over, the one named last changes fastest.
Arguments:
- specimen: float32 [4, 2, 2048, 2048], P('depth', None, 'tile'), may hold values from -4.2 to 4.2
- scan_offsets: int32 [32, 2], P('tile'), may hold values from 0 to 1792, as said below
- probe_wave: float32 [2, 256, 256], replicated, may hold values from -4.2 to 4.2
- fresnel_phase: float32 [256, 256], replicated, may hold values from -3.140625 to 3.140625
- measured: float32 [32, 256, 256], P('tile'), may hold values from 0 to 3
Outputs:
- specimen_gradient: float32 [4, 2, 2048, 2048], P('depth', None, 'tile')
Inputs may be any that keep to these rules, and one draw needn't show every extreme that they name: `scan_offsets`: A position held by tile index d (positions d * 2 to (d + 1) * 2 - 1) has its top row between max(0, (d - 1) * 128) and min(d * 128, 1792), and its left column at most 1792.
All inputs are finite; a program needn't handle non-finite values.
Results may differ from a plain program's by a relative error of at most 0.0003.
Values sent between devices are 32-bit elements; how exact they have to be, the bound alone decides.
No kernel may reach another device: no remote copies, remote signals or barrier semaphores. Data moves between devices by JAX's collectives and lax.ppermute only.
A program may use at most 128 MiB of HBM per device.

v0:
```python
import functools

import jax
import jax.numpy as jnp
import numpy as np
from jax import lax
from jax.experimental import pallas as pl
from jax.experimental.pallas import tpu as pltpu
from jax.sharding import PartitionSpec as P

F32 = jnp.float32
BF16 = jnp.bfloat16
AXES = ("depth", "tile")
ANY = pl.BlockSpec(memory_space=pl.ANY)
VMEM = pl.BlockSpec(memory_space=pltpu.VMEM)
SMEM = pl.BlockSpec(memory_space=pltpu.SMEM)
cat = jnp.concatenate


def dft_tables(extent):
    half = extent // 2
    row, col = np.arange(half)[:, None], np.arange(half)[None, :]
    blocks = []
    for parity in (0, 1):
        turn = (row * (2 * col + parity)) % extent
        wave = np.exp(-2j * np.pi * turn / extent) / np.sqrt(extent)
        blocks.append(np.block([[wave.real, wave.imag], [-wave.imag, wave.real]]))
    table = np.stack([blocks[0], blocks[1], blocks[0].T, blocks[1].T])
    high = table.astype(np.float32).astype(BF16)
    low = (table - high.astype(np.float64)).astype(np.float32).astype(BF16)
    return np.stack([high, low], 1)


def split(x):
    high = x.astype(BF16)
    return high, (x - high.astype(F32)).astype(BF16)


def dot(a, b):
    return jnp.dot(a, b, preferred_element_type=F32)


def rmul(x, table, which):
    high, low = split(x)
    t_high, t_low = table[which, 0], table[which, 1]
    return dot(high, t_high) + (dot(low, t_high) + dot(high, t_low))


def lmul(table, which, x):
    high, low = split(x)
    t_high, t_low = table[which, 0], table[which, 1]
    return dot(t_high, high) + (dot(t_high, low) + dot(t_low, high))


def forward(xr, xi, table):
    h = xr.shape[0] // 2
    e = rmul(cat([xr[:, :h] + xr[:, h:], xi[:, :h] + xi[:, h:]], 1), table, 0)
    o = rmul(cat([xr[:, :h] - xr[:, h:], xi[:, :h] - xi[:, h:]], 1), table, 1)
    yr, yi = cat([e[:, :h], o[:, :h]], 1), cat([e[:, h:], o[:, h:]], 1)
    e = lmul(table, 2, cat([yr[:h] + yr[h:], yi[:h] + yi[h:]], 0))
    o = lmul(table, 3, cat([yr[:h] - yr[h:], yi[:h] - yi[h:]], 0))
    return cat([e[:h], o[:h]], 0), cat([e[h:], o[h:]], 0)


def inverse(xr, xi, table):
    h = xr.shape[0] // 2
    e = lmul(table, 0, cat([xr[:h], xi[:h]], 0))
    o = lmul(table, 1, cat([xr[h:], xi[h:]], 0))
    yr = cat([e[:h] + o[:h], e[:h] - o[:h]], 0)
    yi = cat([e[h:] + o[h:], e[h:] - o[h:]], 0)
    e = rmul(cat([yr[:, :h], yi[:, :h]], 1), table, 2)
    o = rmul(cat([yr[:, h:], yi[:, h:]], 1), table, 3)
    return (
        cat([e[:, :h] + o[:, :h], e[:, :h] - o[:, :h]], 1),
        cat([e[:, h:] + o[:, h:], e[:, h:] - o[:, h:]], 1),
    )


def times(ref, a, b, conj):
    pr, pi = ref[0], ref[1]
    if conj:
        return pr * a + pi * b, pr * b - pi * a
    return pr * a - pi * b, pr * b + pi * a


def extract_kernel(count, cols_ref, *refs):
    blocks, outs = refs[: 2 * count], refs[2 * count :]
    lane = lax.broadcasted_iota(jnp.int32, outs[0].shape[2:], 1)
    for i in range(count):
        shift = cols_ref[i] % outs[0].shape[3]
        outs[i][0, 0] = jnp.where(lane < shift, blocks[2 * i + 1][0, 0], blocks[2 * i][0, 0])


def extract(specimen, cols, patch):
    count = cols.shape[0]
    layers, parts, rows, width = specimen.shape
    last = width // patch - 1

    def spec(i, step):
        def index(s, c, cols_ref):
            return s, c, 0, jnp.minimum(cols_ref[i] // patch + step, last)

        return pl.BlockSpec((1, 1, rows, patch), index)

    out = pl.BlockSpec((1, 1, rows, patch), lambda s, c, cols_ref: (s, c, 0, 0))
    size = layers * parts * rows * patch * 4
    return pl.pallas_call(
        functools.partial(extract_kernel, count),
        out_shape=[jax.ShapeDtypeStruct((layers, parts, rows, patch), F32)] * count,
        grid_spec=pltpu.PrefetchScalarGridSpec(
            num_scalar_prefetch=1,
            grid=(layers, parts),
            in_specs=[spec(i, step) for i in range(count) for step in (0, 1)],
            out_specs=[out] * count,
        ),
        cost_estimate=pl.CostEstimate(
            flops=count * size // 4, bytes_accessed=3 * count * size, transcendentals=0
        ),
        name="extract",
    )(cols, *([specimen] * (2 * count)))


def pick(depth, at_zero, at_one, dst, sem):
    @pl.when(depth == 0)
    def _():
        pltpu.make_async_copy(at_zero, dst, sem).start()

    @pl.when(depth != 0)
    def _():
        pltpu.make_async_copy(at_one, dst, sem).start()

    return pltpu.make_async_copy(at_zero, dst, sem)


def fetch(scal, sources, patches, third, own, sems):
    rows = third.shape[2]
    depth = scal[0]
    lower = patches.at[:, :, pl.ds(rows, rows), :]
    copies = [
        pick(depth, sources[0], sources[1], lower, sems.at[0]),
        pick(depth, sources[2], sources[3], third, sems.at[1]),
        pick(depth, sources[4], sources[5], own, sems.at[2]),
    ]
    return copies


def merge(scal, patches, third, own):
    layers, parts, rows, patch = third.shape
    row = lax.broadcasted_iota(jnp.int32, (rows, patch), 0)
    from_own = (row < scal[2]) == (scal[1] == 1)
    for s in range(layers):
        for c in range(parts):
            patches[s, c, :rows] = jnp.where(from_own, own[s, c], third[s, c])


def first_kernel(scal, probe, kernel, table, *refs):
    sources, refs = refs[:6], refs[6:]
    patches, waves, rolled, third, own, cur, sems = refs
    copies = fetch(scal, sources, patches, third, own, sems)
    patch = probe.shape[-1]
    for c in range(2):
        turned = pltpu.roll(probe[c], scal[2], 0)
        turned = pltpu.roll(turned, scal[3] % patch, 1)
        rolled[c] = turned
        cur[c] = turned
    for copy in copies:
        copy.wait()
    merge(scal, patches, third, own)

    def step(s, unused):
        a, b = times(patches.at[s], cur[0], cur[1], False)
        a, b = forward(a, b, table)
        a, b = times(kernel, a, b, False)
        a, b = inverse(a, b, table)
        cur[0], cur[1] = a, b
        waves[s, 0], waves[s, 1] = a, b
        return unused

    lax.fori_loop(0, patches.shape[0], step, 0)


def put_grad(grad_top, grad_low, s, a, b):
    rows = grad_top.shape[2]
    grad_top[s, 0], grad_top[s, 1] = a[:rows], b[:rows]
    grad_low[s, 0], grad_low[s, 1] = a[rows:], b[rows:]


def second_kernel(scal, kernel, table, target, waves, *refs):
    sources, refs = refs[:6], refs[6:]
    grad_top, grad_low, leaving, patches, third, own, cur, last, sems = refs
    copies = fetch(scal, sources, patches, third, own, sems)
    for copy in copies:
        copy.wait()
    merge(scal, patches, third, own)
    entry = waves.at[1]
    a, b = times(patches.at[0], entry[0], entry[1], False)
    cur[0], cur[1] = a, b

    def step(s, unused):
        a, b = forward(cur[0], cur[1], table)
        middle = s == 1
        residue = 2.0 * (a * a + b * b - target[...])
        kr = jnp.where(middle, residue, kernel[0])
        ki = jnp.where(middle, 0.0, jnp.where(s == 0, kernel[1], -kernel[1]))
        a, b = kr * a - ki * b, kr * b + ki * a
        a, b = inverse(a, b, table)
        cur[0], cur[1] = a, b

        @pl.when(s == 0)
        def _():
            a, b = cur[0], cur[1]
            last[0], last[1] = a, b
            cur[0], cur[1] = times(patches.at[1], a, b, False)

        @pl.when(s == 1)
        def _():
            a, b = cur[0], cur[1]
            put_grad(grad_top, grad_low, 1, *times(last, a, b, True))
            cur[0], cur[1] = times(patches.at[1], a, b, True)

        @pl.when(s == 2)
        def _():
            a, b = cur[0], cur[1]
            put_grad(grad_top, grad_low, 0, *times(entry, a, b, True))
            leaving[0], leaving[1] = times(patches.at[0], a, b, True)

        return unused

    lax.fori_loop(0, 3, step, 0)


def third_kernel(kernel, table, waves, rolled, patches, entering, grad_top, grad_low, cur):
    cur[...] = entering[...]

    def step(s, unused):
        a, b = forward(cur[0], cur[1], table)
        a, b = times(kernel, a, b, True)
        a, b = inverse(a, b, table)
        cur[0], cur[1] = a, b

        @pl.when(s == 0)
        def _():
            a, b = cur[0], cur[1]
            put_grad(grad_top, grad_low, 1, *times(waves.at[0], a, b, True))
            cur[0], cur[1] = times(patches.at[1], a, b, True)

        @pl.when(s == 1)
        def _():
            put_grad(grad_top, grad_low, 0, *times(rolled, cur[0], cur[1], True))

        return unused

    lax.fori_loop(0, 2, step, 0)


def gather_kernel(scal, *refs):
    sources, (out, windows, total, sems, out_sems) = refs[:12], refs[12:]
    count = 6
    layers, parts, rows, patch = windows.shape[1:]
    final = total.shape[3] // patch - 1
    copies = [
        pick(scal[0], sources[2 * i], sources[2 * i + 1], windows.at[i], sems.at[i])
        for i in range(count)
    ]
    row = lax.broadcasted_iota(jnp.int32, (rows, patch), 0)
    lane = lax.broadcasted_iota(jnp.int32, (rows, patch), 1)
    odd = scal[1] == 1
    total[...] = jnp.zeros_like(total)
    for copy in copies:
        copy.wait()
    sends = []
    for s in range(layers):
        for c in range(parts):
            for i in range(count):
                column = scal[2 + 2 * i]
                value = windows[i, s, c]
                if i >= 2:
                    above = row < scal[3 + 2 * i]
                    keep = (above == odd) if i < 4 else (above != odd)
                    value = jnp.where(keep, value, 0.0)
                block, shift = column // patch, column % patch
                near = pl.ds(pl.multiple_of(block * patch, patch), patch)
                far = pl.ds(pl.multiple_of(jnp.minimum(block + 1, final) * patch, patch), patch)
                total[s, c, :, near] += jnp.where(lane < shift, 0.0, value)
                total[s, c, :, far] += jnp.where(lane < shift, value, 0.0)
            copy = pltpu.make_async_copy(total.at[s, c], out.at[s, c], out_sems.at[s, c])
            copy.start()
            sends.append(copy)
    for copy in sends:
        copy.wait()


def local(specimen, scan_offsets, probe_wave, fresnel_phase, measured):
    layers, parts, rows, width = specimen.shape
    patch = probe_wave.shape[-1]
    tiles, depths = lax.axis_size("tile"), lax.axis_size("depth")
    assert depths == 2 and layers == 2 and scan_offsets.shape[0] == depths
    assert tiles % 2 == 0 and patch == 2 * rows and width % patch == 0
    tile, depth = lax.axis_index("tile"), lax.axis_index("depth")
    parity = tile % 2

    swap = [(t, t ^ 1) for t in range(tiles)]
    other = [(t, t + 1) for t in range(1, tiles - 1, 2)] + [(t, t - 1) for t in range(2, tiles, 2)]
    outward = [(t, t + 2) for t in range(1, tiles - 2, 2)] + [
        (t, t - 2) for t in range(2, tiles, 2)
    ]
    homeward = [(b, a) for a, b in outward]
    stay = [(t, t) for t in range(tiles)]

    def send(value, pairs, *hops):
        return lax.ppermute(
            value, AXES, [(a * tiles + s, b * tiles + t) for a, b in hops for s, t in pairs]
        )

    their = lax.ppermute(scan_offsets, "tile", other)
    partner = lax.ppermute(scan_offsets, "tile", swap)
    target = lax.ppermute(
        lax.dynamic_index_in_dim(measured, depth, 0, keepdims=False), "tile", swap
    )
    order = jnp.stack([depth, 1 - depth])
    own_cols = scan_offsets[order, 1]
    their_cols, their_rows = their[order, 1], their[order, 0]
    part_cols, part_rows = partner[order, 1], partner[order, 0]
    part_rows = part_rows - ((tile ^ 1) - 1) * rows
    their_tile = jnp.where(parity == 1, tile + 1, tile - 1)
    their_rows = their_rows - (their_tile - 1) * rows

    table = jnp.asarray(dft_tables(patch))
    places = np.concatenate([np.arange(0, patch, 2), np.arange(1, patch, 2)])
    pick_one = jnp.asarray(np.eye(patch, dtype=np.float32)[places])

    def reorder(x):
        x = jnp.dot(pick_one, x, precision=lax.Precision.HIGHEST)
        return jnp.dot(x, pick_one.T, precision=lax.Precision.HIGHEST)

    phase = reorder(fresnel_phase)
    kernel = jnp.stack([jnp.cos(phase), jnp.sin(phase)], 0)
    target = reorder(target)

    mid_keep, mid_swap = extract(specimen, own_cols, patch)
    mids = [
        send(mid_keep, swap, (0, 0)),
        send(mid_swap, swap, (0, 1)),
    ]
    far_keep, far_swap, near_keep, near_swap = extract(
        specimen, cat([their_cols, part_cols]), patch
    )
    fars = [
        send(far_keep, outward, (0, 0)),
        send(far_swap, outward, (0, 1)),
    ]
    near_other = send(near_swap, stay, (0, 1), (1, 0))
    mids += [send(mid_swap, swap, (1, 0)), send(mid_keep, swap, (1, 1))]
    fars += [send(far_swap, outward, (1, 0)), send(far_keep, outward, (1, 1))]

    scal = jnp.stack([depth, parity, part_rows[0], part_cols[0]]).astype(jnp.int32)
    pair = jax.ShapeDtypeStruct((2, patch, patch), F32)
    slab = jax.ShapeDtypeStruct((layers, 2, patch, patch), F32)
    band = jax.ShapeDtypeStruct((layers, 2, rows, patch), F32)
    full_v = pltpu.VMEM((layers, 2, patch, patch), F32)
    band_v = pltpu.VMEM((layers, 2, rows, patch), F32)
    pair_v = pltpu.VMEM((2, patch, patch), F32)
    work = 12 * 2 * patch**3
    patches, waves, rolled = pl.pallas_call(
        first_kernel,
        out_shape=[slab, slab, pair],
        in_specs=[SMEM, VMEM, VMEM, VMEM] + [ANY] * 6,
        out_specs=[VMEM] * 3,
        scratch_shapes=[band_v, band_v, pair_v, pltpu.SemaphoreType.DMA((3,))],
        cost_estimate=pl.CostEstimate(flops=4 * work, bytes_accessed=6 << 20, transcendentals=0),
        name="first",
    )(scal, probe_wave, kernel, table, mids[0], mids[1], fars[0], fars[1], near_keep, near_other)
    top_b, low_b, leaving = pl.pallas_call(
        second_kernel,
        out_shape=[band, band, pair],
        in_specs=[SMEM, VMEM, VMEM, VMEM, VMEM] + [ANY] * 6,
        out_specs=[VMEM] * 3,
        scratch_shapes=[full_v, band_v, band_v, pair_v, pair_v, pltpu.SemaphoreType.DMA((3,))],
        cost_estimate=pl.CostEstimate(flops=6 * work, bytes_accessed=6 << 20, transcendentals=0),
        name="second",
    )(scal, kernel, table, target, waves, mids[2], mids[3], fars[2], fars[3], near_other, near_keep)
    low_back = [None, send(low_b, swap, (1, 1)), None, send(low_b, swap, (0, 1))]
    top_back = [None, send(top_b, homeward, (1, 1)), None, send(top_b, homeward, (0, 1))]
    top_b_other = send(top_b, stay, (0, 1))
    top_c, low_c = pl.pallas_call(
        third_kernel,
        out_shape=[band, band],
        in_specs=[VMEM] * 6,
        out_specs=[VMEM] * 2,
        scratch_shapes=[pair_v],
        cost_estimate=pl.CostEstimate(flops=4 * work, bytes_accessed=6 << 20, transcendentals=0),
        name="third",
    )(kernel, table, waves, rolled, patches, leaving)
    low_back[0], low_back[2] = send(low_c, swap, (0, 0)), send(low_c, swap, (1, 0))
    top_back[0], top_back[2] = send(top_c, homeward, (0, 0)), send(top_c, homeward, (1, 0))
    top_c_other = send(top_c, stay, (1, 0))

    zero = jnp.zeros((), jnp.int32)
    places = jnp.stack(
        [depth, parity]
        + [own_cols[0], zero, own_cols[1], zero]
        + [part_cols[0], part_rows[0], part_cols[1], part_rows[1]]
        + [their_cols[0], their_rows[0], their_cols[1], their_rows[1]]
    ).astype(jnp.int32)
    return pl.pallas_call(
        gather_kernel,
        out_shape=jax.ShapeDtypeStruct(specimen.shape, F32),
        in_specs=[SMEM] + [ANY] * 12,
        out_specs=ANY,
        scratch_shapes=[
            pltpu.VMEM((6, layers, 2, rows, patch), F32),
            pltpu.VMEM(specimen.shape, F32),
            pltpu.SemaphoreType.DMA((6,)),
            pltpu.SemaphoreType.DMA((layers, 2)),
        ],
        cost_estimate=pl.CostEstimate(flops=6 << 20, bytes_accessed=7 << 20, transcendentals=0),
        name="gather",
    )(places, *low_back, top_c, top_b, top_c_other, top_b_other, *top_back)


def solution(mesh):
    placed = (P("depth", None, "tile", None), P("tile", None), P(), P(), P("tile", None, None))
    return jax.shard_map(
        local, mesh=mesh, in_specs=placed, out_specs=P("depth", None, "tile", None), check_vma=False
    )
```

profile of v0, /device:TPU:0, one launch (start us, length us, event | category | flops | bytes accessed | tf_op | source)
XLA Modules:
  0.0 117.2 jit_solution(8781533331927695680)
XLA Ops:
  0.0 0.8 collective-permute-start.1
  0.8 5.8 %collective-permute-start = (s32[2,2]{1,0:T(2,128)}, s32[2,2]{1,0:T(2,128)S(1)}, u32[]{:S(2)}, u32[]{:S(2)}) collective-permute-start(s32[2,2]{1,0:T(2,128)} %param.8), channel_id=1, source_target_pairs={{0,1},{1,0},{2,3},{3,2},{4,5},{5,4},{6,7},{7,6},{8,9},{9,8},{10,11... | collective-permute-start | bytes 56 | tf_op jit(solution)/shard_map/ppermute | solution.py:316
  6.8 1.9 %gather_fusion = s32[2]{0:T(128)} fusion(s32[2,2]{1,0:T(2,128)} %param.8, s32[2]{0:T(128)S(1)} %get-tuple-element.33), kind=kCustom, calls=%fused_computation | custom fusion | bytes 32 | tf_op jit(solution)/shard_map/gather | solution.py:321
  8.7 4.5 %extract.2 = (f32[2,2,128,256]{3,2,1,0:T(8,128)}, f32[2,2,128,256]{3,2,1,0:T(8,128)}) custom-call(s32[2]{0:T(128)} %gather_fusion, f32[2,2,128,2048]{3,2,1,0:T(8,128)} %refs_7_.1, f32[2,2,128,2048]{3,2,1,0:T(8,128)} %refs_7_.1, f32[2,2,128,2048]{3,2,1,0:T(8,128)} %refs_7_.1, f32[2,2,128,2048]{3,2,1,0:T(8,128)} %refs_7_.1), custom_call_target="tpu_custom_call" | custom-call | flops 262144 | bytes 3145728 | tf_op jit(solution)/shard_map/extract/pallas_call | solution.py:107
  13.2 3.9 %collective-permute-start.2 = (f32[2,2,128,256]{3,2,1,0:T(8,128)}, f32[2,2,128,256]{3,2,1,0:T(8,128)}, u32[]{:S(2)}, u32[]{:S(2)}) collective-permute-start(f32[2,2,128,256]{3,2,1,0:T(8,128)} %get-tuple-element.19), channel_id=1, source_target_pairs={{0,1},{1,0},{2,3},{3,2},{4,5},{5,4},{6,7},{7,6},{8,9},{9,8},{10,11... | collective-permute-start | bytes 1572872 | tf_op jit(solution)/shard_map/ppermute | solution.py:311
  17.0 2.1 %collective-permute-start.3 = (f32[2,2,128,256]{3,2,1,0:T(8,128)}, f32[2,2,128,256]{3,2,1,0:T(8,128)}, u32[]{:S(2)}, u32[]{:S(2)}) collective-permute-start(f32[2,2,128,256]{3,2,1,0:T(8,128)} %get-tuple-element.20), channel_id=1, source_target_pairs={{0,17},{1,16},{2,19},{3,18},{4,21},{5,20},{6,23},{7,22},{8,25},{9,... | collective-permute-start | bytes 1572872 | tf_op jit(solution)/shard_map/ppermute | solution.py:311
  19.1 0.4 fusion.8
  19.5 1.7 %cosine_bitcast_fusion = (f32[1,256,256]{2,1,0:T(8,128)S(1)}, f32[1,256,256]{2,1,0:T(8,128)S(1)}) fusion(f32[256,256]{1,0:T(8,128)S(1)} %fusion.8, f32[256,256]{1,0:T(8,128)S(1)} %copy-done.1), kind=kOutput, calls=%fused_computation.8 | convolution fusion | flops 201326592 | bytes 1048576 | tf_op jit(solution)/shard_map/dot_general | solution.py:334
  21.3 0.8 pad_maximum_fusion.kernel
  22.1 0.6 gather_fusion.3
  22.7 0.6 gather_fusion.1
  23.4 0.7 pad_add_fusion.1.cols_ref
  24.1 5.2 %extract.3 = (f32[2,2,128,256]{3,2,1,0:T(8,128)}, f32[2,2,128,256]{3,2,1,0:T(8,128)}, f32[2,2,128,256]{3,2,1,0:T(8,128)}, f32[2,2,128,256]{3,2,1,0:T(8,128)}) custom-call(s32[4]{0:T(128)} %pad_add_fusion.1.cols_ref, f32[2,2,128,2048]{3,2,1,0:T(8,128)} %refs_7_.1, f32[2,2,128,2048]{3,2,1,0:T(8,128)} %refs_7_.1, f32[2,2,128,2048]{3,2,1,0:T(8,128)} %refs_7_.1, ...), custom_call_target="tpu_custom_call" | custom-call | flops 524288 | bytes 6291456 | tf_op jit(solution)/shard_map/extract/pallas_call | solution.py:107
  29.3 1.3 %collective-permute-start.4 = (f32[2,2,128,256]{3,2,1,0:T(8,128)}, f32[2,2,128,256]{3,2,1,0:T(8,128)S(1)}, u32[]{:S(2)}, u32[]{:S(2)}) collective-permute-start(f32[2,2,128,256]{3,2,1,0:T(8,128)} %get-tuple-element.21), channel_id=1, source_target_pairs={{1,3},{3,5},{5,7},{7,9},{9,11},{11,13},{13,15},{2,0},{4,2},{6,4},{... | collective-permute-start | bytes 1572872 | tf_op jit(solution)/shard_map/ppermute | solution.py:311
  30.6 0.6 gather_fusion.2
  31.3 0.6 fusion.6
  31.9 0.6 fusion.5
  32.6 1.5 %collective-permute-start.5 = (f32[2,2,128,256]{3,2,1,0:T(8,128)}, f32[2,2,128,256]{3,2,1,0:T(8,128)}, u32[]{:S(2)}, u32[]{:S(2)}) collective-permute-start(f32[2,2,128,256]{3,2,1,0:T(8,128)} %get-tuple-element.22), channel_id=1, source_target_pairs={{1,19},{3,21},{5,23},{7,25},{9,27},{11,29},{13,31},{2,16},{4,18},{... | collective-permute-start | bytes 1572872 | tf_op jit(solution)/shard_map/ppermute | solution.py:311
  34.1 1.9 %pad_add_fusion.scal = s32[4]{0:T(128)} fusion(s32[1]{0:T(128)} %get-tuple-element.44, s32[1]{0:T(128)} %get-tuple-element.42, s32[1]{0:T(128)} %bitcast.1, s32[1]{0:T(128)} %bitcast), kind=kLoop, calls=%fused_computation.12 | loop fusion | flops 12 | bytes 32 | tf_op jit(solution)/shard_map/stack | solution.py:356
  36.0 1.5 %collective-permute-start.9 = (f32[2,2,128,256]{3,2,1,0:T(8,128)S(1)}, f32[2,2,128,256]{3,2,1,0:T(8,128)}, u32[]{:S(2)}, u32[]{:S(2)}) collective-permute-start(f32[2,2,128,256]{3,2,1,0:T(8,128)S(1)} %copy-done.10), channel_id=1, source_target_pairs={{16,17},{17,16},{18,19},{19,18},{20,21},{21,20},{22,23},{23,22},{2... | collective-permute-start | bytes 1572872 | tf_op jit(solution)/shard_map/ppermute | solution.py:311
  37.5 1.3 %collective-permute-start.8 = (f32[2,2,128,256]{3,2,1,0:T(8,128)S(1)}, f32[2,2,128,256]{3,2,1,0:T(8,128)}, u32[]{:S(2)}, u32[]{:S(2)}) collective-permute-start(f32[2,2,128,256]{3,2,1,0:T(8,128)S(1)} %copy-done.9), channel_id=1, source_target_pairs={{16,1},{17,0},{18,3},{19,2},{20,5},{21,4},{22,7},{23,6},{24,9},{25... | collective-permute-start | bytes 1572872 | tf_op jit(solution)/shard_map/ppermute | solution.py:311
  38.8 1.5 %collective-permute-start.11 = (f32[2,2,128,256]{3,2,1,0:T(8,128)}, f32[2,2,128,256]{3,2,1,0:T(8,128)}, u32[]{:S(2)}, u32[]{:S(2)}) collective-permute-start(f32[2,2,128,256]{3,2,1,0:T(8,128)} %get-tuple-element.21), channel_id=1, source_target_pairs={{17,19},{19,21},{21,23},{23,25},{25,27},{27,29},{29,31},{18,16},{2... | collective-permute-start | bytes 1572872 | tf_op jit(solution)/shard_map/ppermute | solution.py:311
  40.2 0.4 collective-permute-done.4.refs_2_
  40.6 1.3 %collective-permute-start.10 = (f32[2,2,128,256]{3,2,1,0:T(8,128)}, f32[2,2,128,256]{3,2,1,0:T(8,128)}, u32[]{:S(2)}, u32[]{:S(2)}) collective-permute-start(f32[2,2,128,256]{3,2,1,0:T(8,128)} %get-tuple-element.22), channel_id=1, source_target_pairs={{17,3},{19,5},{21,7},{23,9},{25,11},{27,13},{29,15},{18,0},{20,2},... | collective-permute-start | bytes 1572872 | tf_op jit(solution)/shard_map/ppermute | solution.py:311
  41.9 0.6 fusion.9
  42.5 1.3 %fusion.10.target = f32[256,256]{1,0:T(8,128)} fusion(f32[256,256]{1,0:T(8,128)S(1)} %fusion.9, f32[256,256]{1,0:T(8,128)S(1)} %copy-done.1), kind=kOutput, calls=%fused_computation.24 | convolution fusion | flops 201326592 | bytes 786432 | tf_op jit(solution)/shard_map/dot_general | solution.py:334
  43.9 7.3 %first.1 = (f32[2,2,256,256]{3,2,1,0:T(8,128)}, f32[2,2,256,256]{3,2,1,0:T(8,128)}, f32[2,256,256]{2,1,0:T(8,128)}) custom-call(s32[4]{0:T(128)} %pad_add_fusion.scal, f32[2,256,256]{2,1,0:T(8,128)} %probe.1, f32[2,256,256]{2,1,0:T(8,128)} %pad_maximum_fusion.kernel, bf16[4,2,256,256]{3,2,1,0:T(8,128)(2,1)} %constant.43.clone.table, ...), custom_call_target="tpu_custom_call" | custom-call | flops 1610612736 | bytes 6291456 | tf_op jit(solution)/shard_map/first/pallas_call | solution.py:364
  51.2 0.3 collective-permute-done.8.refs_0_
  51.5 8.8 %collective-permute-done.10.refs_2_ = f32[2,2,128,256]{3,2,1,0:T(8,128)} collective-permute-done((f32[2,2,128,256]{3,2,1,0:T(8,128)}, f32[2,2,128,256]{3,2,1,0:T(8,128)}, u32[]{:S(2)}, u32[]{:S(2)}) %collective-permute-start.10) | collective-permute-done | bytes 524320 | tf_op jit(solution)/shard_map/ppermute | solution.py:311
  60.2 9.5 %second.1 = (f32[2,2,128,256]{3,2,1,0:T(8,128)}, f32[2,2,128,256]{3,2,1,0:T(8,128)}, f32[2,256,256]{2,1,0:T(8,128)}) custom-call(s32[4]{0:T(128)} %pad_add_fusion.scal, f32[2,256,256]{2,1,0:T(8,128)} %pad_maximum_fusion.kernel, bf16[4,2,256,256]{3,2,1,0:T(8,128)(2,1)} %constant.43.clone.table, f32[256,256]{1,0:T(8,128)} %fusion.10.target, ...), custom_call_target="tpu_custom_call" | custom-call | flops 2415919104 | bytes 6291456 | tf_op jit(solution)/shard_map/second/pallas_call | solution.py:373
  69.8 6.5 %third.1 = (f32[2,2,128,256]{3,2,1,0:T(8,128)}, f32[2,2,128,256]{3,2,1,0:T(8,128)}) custom-call(f32[2,256,256]{2,1,0:T(8,128)} %pad_maximum_fusion.kernel, bf16[4,2,256,256]{3,2,1,0:T(8,128)(2,1)} %constant.43.clone.table, f32[2,2,256,256]{3,2,1,0:T(8,128)} %get-tuple-element.25.waves, f32[2,256,256]{2,1,0:T(8,128)} %get-tuple-element.26.rolled, ...), custom_call_target="tpu_custom_call" | custom-call | flops 1610612736 | bytes 6291456 | tf_op jit(solution)/shard_map/third/pallas_call | solution.py:385
  76.3 1.3 %collective-permute-start.14 = (f32[2,2,128,256]{3,2,1,0:T(8,128)}, f32[2,2,128,256]{3,2,1,0:T(8,128)S(1)}, u32[]{:S(2)}, u32[]{:S(2)}) collective-permute-start(f32[2,2,128,256]{3,2,1,0:T(8,128)} %get-tuple-element.29), channel_id=1, source_target_pairs={{16,1},{17,0},{18,3},{19,2},{20,5},{21,4},{22,7},{23,6},{24,9},{25... | collective-permute-start | bytes 1572872 | tf_op jit(solution)/shard_map/ppermute | solution.py:311
  77.6 1.9 %collective-permute-start.12 = (f32[2,2,128,256]{3,2,1,0:T(8,128)}, f32[2,2,128,256]{3,2,1,0:T(8,128)S(1)}, u32[]{:S(2)}, u32[]{:S(2)}) collective-permute-start(f32[2,2,128,256]{3,2,1,0:T(8,128)} %get-tuple-element.29), channel_id=1, source_target_pairs={{0,1},{1,0},{2,3},{3,2},{4,5},{5,4},{6,7},{7,6},{8,9},{9,8},{10,11... | collective-permute-start | bytes 1572872 | tf_op jit(solution)/shard_map/ppermute | solution.py:311
  79.5 0.7 collective-permute-start.20
  80.2 5.1 %collective-permute-start.18 = (f32[2,2,128,256]{3,2,1,0:T(8,128)}, f32[2,2,128,256]{3,2,1,0:T(8,128)S(1)}, u32[]{:S(2)}, u32[]{:S(2)}) collective-permute-start(f32[2,2,128,256]{3,2,1,0:T(8,128)} %get-tuple-element.31.refs_4_), channel_id=1, source_target_pairs={{3,1},{5,3},{7,5},{9,7},{11,9},{13,11},{15,13},{0,2},{2,4},{4,6},{... | collective-permute-start | bytes 1572872 | tf_op jit(solution)/shard_map/ppermute | solution.py:311
  85.4 1.3 %collective-permute-start.16 = (f32[2,2,128,256]{3,2,1,0:T(8,128)}, f32[2,2,128,256]{3,2,1,0:T(8,128)}, u32[]{:S(2)}, u32[]{:S(2)}) collective-permute-start(f32[2,2,128,256]{3,2,1,0:T(8,128)} %get-tuple-element.31.refs_4_), channel_id=1, source_target_pairs={{16,0},{17,1},{18,2},{19,3},{20,4},{21,5},{22,6},{23,7},{24,8},{25... | collective-permute-start | bytes 1572872 | tf_op jit(solution)/shard_map/ppermute | solution.py:311
  86.7 4.1 %collective-permute-done.14.refs_2_ = f32[2,2,128,256]{3,2,1,0:T(8,128)S(1)} collective-permute-done((f32[2,2,128,256]{3,2,1,0:T(8,128)}, f32[2,2,128,256]{3,2,1,0:T(8,128)S(1)}, u32[]{:S(2)}, u32[]{:S(2)}) %collective-permute-start.14) | collective-permute-done | bytes 524320 | tf_op jit(solution)/shard_map/ppermute | solution.py:311
  90.8 2.1 %collective-permute-start.15 = (f32[2,2,128,256]{3,2,1,0:T(8,128)}, f32[2,2,128,256]{3,2,1,0:T(8,128)}, u32[]{:S(2)}, u32[]{:S(2)}) collective-permute-start(f32[2,2,128,256]{3,2,1,0:T(8,128)} %get-tuple-element.30), channel_id=1, source_target_pairs={{0,17},{1,16},{2,19},{3,18},{4,21},{5,20},{6,23},{7,22},{8,25},{9,... | collective-permute-start | bytes 1572872 | tf_op jit(solution)/shard_map/ppermute | solution.py:311
  92.9 1.5 %collective-permute-start.13 = (f32[2,2,128,256]{3,2,1,0:T(8,128)}, f32[2,2,128,256]{3,2,1,0:T(8,128)}, u32[]{:S(2)}, u32[]{:S(2)}) collective-permute-start(f32[2,2,128,256]{3,2,1,0:T(8,128)} %get-tuple-element.30), channel_id=1, source_target_pairs={{16,17},{17,16},{18,19},{19,18},{20,21},{21,20},{22,23},{23,22},{2... | collective-permute-start | bytes 1572872 | tf_op jit(solution)/shard_map/ppermute | solution.py:311
  94.3 4.3 %collective-permute-start.21 = (f32[2,2,128,256]{3,2,1,0:T(8,128)S(1)}, f32[2,2,128,256]{3,2,1,0:T(8,128)}, u32[]{:S(2)}, u32[]{:S(2)}) collective-permute-start(f32[2,2,128,256]{3,2,1,0:T(8,128)S(1)} %copy-done.2), channel_id=1, source_target_pairs={{3,17},{5,19},{7,21},{9,23},{11,25},{13,27},{15,29},{0,18},{2,20},... | collective-permute-start | bytes 1572872 | tf_op jit(solution)/shard_map/ppermute | solution.py:311
  98.7 1.5 %collective-permute-start.19 = (f32[2,2,128,256]{3,2,1,0:T(8,128)S(1)}, f32[2,2,128,256]{3,2,1,0:T(8,128)}, u32[]{:S(2)}, u32[]{:S(2)}) collective-permute-start(f32[2,2,128,256]{3,2,1,0:T(8,128)S(1)} %copy-done.2), channel_id=1, source_target_pairs={{19,17},{21,19},{23,21},{25,23},{27,25},{29,27},{31,29},{16,18},{1... | collective-permute-start | bytes 1572872 | tf_op jit(solution)/shard_map/ppermute | solution.py:311
  100.1 2.7 %collective-permute-start.17 = (f32[2,2,128,256]{3,2,1,0:T(8,128)S(1)}, f32[2,2,128,256]{3,2,1,0:T(8,128)}, u32[]{:S(2)}, u32[]{:S(2)}) collective-permute-start(f32[2,2,128,256]{3,2,1,0:T(8,128)S(1)} %copy-done.2), channel_id=1, source_target_pairs={{0,16},{1,17},{2,18},{3,19},{4,20},{5,21},{6,22},{7,23},{8,24},{9,... | collective-permute-start | bytes 1572872 | tf_op jit(solution)/shard_map/ppermute | solution.py:311
  102.8 0.6 fusion.7
  103.4 0.6 gather_fusion.4
  104.0 0.6 fusion.4
  104.7 0.6 fusion.3
  105.3 7.0 %stack.37.scal = s32[14]{0:T(128)} concatenate(s32[1]{0:T(128)} %bitcast, s32[1]{0:T(128)} %bitcast.1, s32[1]{0:T(128)} %get-tuple-element.46, s32[1]{0:T(128)} %constant.40.clone.1, s32[1]{0:T(128)} %get-tuple-element.45, s32[1]{0:T(128)} %constant.40.clone.1, s32[1]{0:T(128)} %get-tuple-element.44, s32[1]{0:T(128)} %get-tuple-element.42, s32[1]{0:T(128)} %get-tuple-element.43, ...), dimensions={0} | concatenate | bytes 112 | tf_op jit(solution)/shard_map/stack | solution.py:399
  112.4 4.8 %gather.26 = f32[2,2,128,2048]{3,2,1,0:T(8,128)} custom-call(s32[14]{0:T(128)} %stack.37.scal, f32[2,2,128,256]{3,2,1,0:T(8,128)} %copy-done.4, f32[2,2,128,256]{3,2,1,0:T(8,128)} %collective-permute-done.13.refs_1_, f32[2,2,128,256]{3,2,1,0:T(8,128)} %copy-done.3, f32[2,2,128,256]{3,2,1,0:T(8,128)} %collective-permute-done.15.refs_3_, ...), custom_call_target="tpu_custom_call" | custom-call | flops 6291456 | bytes 7340032 | tf_op jit(solution)/shard_map/gather/pallas_call | solution.py:405
  (50 shorter events, 0.4 us)
Async XLA Ops:
  0.0 6.6 %copy-start = (f32[2,256,256]{2,1,0:T(8,128)S(1)}, f32[2,256,256]{2,1,0:T(8,128)}, u32[]{:S(2)}) copy-start(f32[2,256,256]{2,1,0:T(8,128)} %param.11) | copy-start | bytes 1572868
  0.0 22.1 %collective-permute-start.1 = (s32[2,2]{1,0:T(2,128)}, s32[2,2]{1,0:T(2,128)S(1)}, u32[]{:S(2)}, u32[]{:S(2)}) collective-permute-start(s32[2,2]{1,0:T(2,128)} %param.8), channel_id=1, source_target_pairs={{1,2},{3,4},{5,6},{7,8},{9,10},{11,12},{13,14},{2,1},{4,3},{6,5},{... | collective-permute-start | bytes 56 | tf_op jit(solution)/shard_map/ppermute | solution.py:315
  0.8 21.9 %collective-permute-start = (s32[2,2]{1,0:T(2,128)}, s32[2,2]{1,0:T(2,128)S(1)}, u32[]{:S(2)}, u32[]{:S(2)}) collective-permute-start(s32[2,2]{1,0:T(2,128)} %param.8), channel_id=1, source_target_pairs={{0,1},{1,0},{2,3},{3,2},{4,5},{5,4},{6,7},{7,6},{8,9},{9,8},{10,11... | collective-permute-start | bytes 56 | tf_op jit(solution)/shard_map/ppermute | solution.py:316
  6.6 26.0 %collective-permute-start.7 = (f32[256,256]{1,0:T(8,128)S(1)}, f32[256,256]{1,0:T(8,128)S(1)}, u32[]{:S(2)}, u32[]{:S(2)}) collective-permute-start(f32[256,256]{1,0:T(8,128)S(1)} %dynamic-slice_bitcast_fusion), channel_id=1, source_target_pairs={{0,1},{1,0},{2,3},{3,2},{4,5},{5,4},{6,7},{7,6},{8,9},{9,8},{10,11... | collective-permute-start | bytes 786440 | tf_op jit(solution)/shard_map/ppermute | solution.py:317
  8.7 10.5 %copy-start.1 = (f32[256,256]{1,0:T(8,128)S(1)}, f32[256,256]{1,0:T(8,128)}, u32[]{:S(2)}) copy-start(f32[256,256]{1,0:T(8,128)} %constant.44.clone) | copy-start | bytes 786436
  8.7 10.5 %copy-start.7 = (f32[256,256]{1,0:T(8,128)S(1)}, f32[256,256]{1,0:T(8,128)}, u32[]{:S(2)}) copy-start(f32[256,256]{1,0:T(8,128)} %param.10) | copy-start | bytes 786436
  13.2 22.8 %collective-permute-start.2 = (f32[2,2,128,256]{3,2,1,0:T(8,128)}, f32[2,2,128,256]{3,2,1,0:T(8,128)}, u32[]{:S(2)}, u32[]{:S(2)}) collective-permute-start(f32[2,2,128,256]{3,2,1,0:T(8,128)} %get-tuple-element.19), channel_id=1, source_target_pairs={{0,1},{1,0},{2,3},{3,2},{4,5},{5,4},{6,7},{7,6},{8,9},{9,8},{10,11... | collective-permute-start | bytes 1572872 | tf_op jit(solution)/shard_map/ppermute | solution.py:311
  17.0 20.4 %collective-permute-start.3 = (f32[2,2,128,256]{3,2,1,0:T(8,128)}, f32[2,2,128,256]{3,2,1,0:T(8,128)}, u32[]{:S(2)}, u32[]{:S(2)}) collective-permute-start(f32[2,2,128,256]{3,2,1,0:T(8,128)} %get-tuple-element.20), channel_id=1, source_target_pairs={{0,17},{1,16},{2,19},{3,18},{4,21},{5,20},{6,23},{7,22},{8,25},{9,... | collective-permute-start | bytes 1572872 | tf_op jit(solution)/shard_map/ppermute | solution.py:311
  24.1 11.9 %copy-start.10 = (f32[2,2,128,256]{3,2,1,0:T(8,128)S(1)}, f32[2,2,128,256]{3,2,1,0:T(8,128)}, u32[]{:S(2)}) copy-start(f32[2,2,128,256]{3,2,1,0:T(8,128)} %get-tuple-element.19) | copy-start | bytes 1572868
  24.1 13.4 %copy-start.9 = (f32[2,2,128,256]{3,2,1,0:T(8,128)S(1)}, f32[2,2,128,256]{3,2,1,0:T(8,128)}, u32[]{:S(2)}) copy-start(f32[2,2,128,256]{3,2,1,0:T(8,128)} %get-tuple-element.20) | copy-start | bytes 1572868
  29.3 9.5 %collective-permute-start.6 = (f32[2,2,128,256]{3,2,1,0:T(8,128)}, f32[2,2,128,256]{3,2,1,0:T(8,128)S(1)}, u32[]{:S(2)}, u32[]{:S(2)}) collective-permute-start(f32[2,2,128,256]{3,2,1,0:T(8,128)} %get-tuple-element.24), channel_id=1, source_target_pairs={{0,16},{1,17},{2,18},{3,19},{4,20},{5,21},{6,22},{7,23},{8,24},{9,... | collective-permute-start | bytes 1572872 | tf_op jit(solution)/shard_map/ppermute | solution.py:311
  29.3 11.3 %collective-permute-start.4 = (f32[2,2,128,256]{3,2,1,0:T(8,128)}, f32[2,2,128,256]{3,2,1,0:T(8,128)S(1)}, u32[]{:S(2)}, u32[]{:S(2)}) collective-permute-start(f32[2,2,128,256]{3,2,1,0:T(8,128)} %get-tuple-element.21), channel_id=1, source_target_pairs={{1,3},{3,5},{5,7},{7,9},{9,11},{11,13},{13,15},{2,0},{4,2},{6,4},{... | collective-permute-start | bytes 1572872 | tf_op jit(solution)/shard_map/ppermute | solution.py:311
  32.6 11.3 %collective-permute-start.5 = (f32[2,2,128,256]{3,2,1,0:T(8,128)}, f32[2,2,128,256]{3,2,1,0:T(8,128)}, u32[]{:S(2)}, u32[]{:S(2)}) collective-permute-start(f32[2,2,128,256]{3,2,1,0:T(8,128)} %get-tuple-element.22), channel_id=1, source_target_pairs={{1,19},{3,21},{5,23},{7,25},{9,27},{11,29},{13,31},{2,16},{4,18},{... | collective-permute-start | bytes 1572872 | tf_op jit(solution)/shard_map/ppermute | solution.py:311
  36.0 15.2 %collective-permute-start.9 = (f32[2,2,128,256]{3,2,1,0:T(8,128)S(1)}, f32[2,2,128,256]{3,2,1,0:T(8,128)}, u32[]{:S(2)}, u32[]{:S(2)}) collective-permute-start(f32[2,2,128,256]{3,2,1,0:T(8,128)S(1)} %copy-done.10), channel_id=1, source_target_pairs={{16,17},{17,16},{18,19},{19,18},{20,21},{21,20},{22,23},{23,22},{2... | collective-permute-start | bytes 1572872 | tf_op jit(solution)/shard_map/ppermute | solution.py:311
  37.5 14.0 %collective-permute-start.8 = (f32[2,2,128,256]{3,2,1,0:T(8,128)S(1)}, f32[2,2,128,256]{3,2,1,0:T(8,128)}, u32[]{:S(2)}, u32[]{:S(2)}) collective-permute-start(f32[2,2,128,256]{3,2,1,0:T(8,128)S(1)} %copy-done.9), channel_id=1, source_target_pairs={{16,1},{17,0},{18,3},{19,2},{20,5},{21,4},{22,7},{23,6},{24,9},{25... | collective-permute-start | bytes 1572872 | tf_op jit(solution)/shard_map/ppermute | solution.py:311
  38.8 5.1 %copy-start.11 = (f32[2,2,128,256]{3,2,1,0:T(8,128)}, f32[2,2,128,256]{3,2,1,0:T(8,128)S(1)}, u32[]{:S(2)}) copy-start(f32[2,2,128,256]{3,2,1,0:T(8,128)S(1)} %collective-permute-done.6.refs_5_.refs_4_) | copy-start | bytes 1572868
  38.8 12.7 %collective-permute-start.11 = (f32[2,2,128,256]{3,2,1,0:T(8,128)}, f32[2,2,128,256]{3,2,1,0:T(8,128)}, u32[]{:S(2)}, u32[]{:S(2)}) collective-permute-start(f32[2,2,128,256]{3,2,1,0:T(8,128)} %get-tuple-element.21), channel_id=1, source_target_pairs={{17,19},{19,21},{21,23},{23,25},{25,27},{27,29},{29,31},{18,16},{2... | collective-permute-start | bytes 1572872 | tf_op jit(solution)/shard_map/ppermute | solution.py:311
  40.6 3.2 %copy-start.12 = (f32[2,2,128,256]{3,2,1,0:T(8,128)}, f32[2,2,128,256]{3,2,1,0:T(8,128)S(1)}, u32[]{:S(2)}) copy-start(f32[2,2,128,256]{3,2,1,0:T(8,128)S(1)} %collective-permute-done.4.refs_2_) | copy-start | bytes 1572868
  40.6 19.6 %collective-permute-start.10 = (f32[2,2,128,256]{3,2,1,0:T(8,128)}, f32[2,2,128,256]{3,2,1,0:T(8,128)}, u32[]{:S(2)}, u32[]{:S(2)}) collective-permute-start(f32[2,2,128,256]{3,2,1,0:T(8,128)} %get-tuple-element.22), channel_id=1, source_target_pairs={{17,3},{19,5},{21,7},{23,9},{25,11},{27,13},{29,15},{18,0},{20,2},... | collective-permute-start | bytes 1572872 | tf_op jit(solution)/shard_map/ppermute | solution.py:311
  69.8 24.6 %copy-start.2 = (f32[2,2,128,256]{3,2,1,0:T(8,128)S(1)}, f32[2,2,128,256]{3,2,1,0:T(8,128)}, u32[]{:S(2)}) copy-start(f32[2,2,128,256]{3,2,1,0:T(8,128)} %get-tuple-element.32.refs_5_) | copy-start | bytes 1572868
  69.8 33.1 %copy-start.8 = (s32[2]{0:T(128)S(1)}, s32[2]{0:T(128)}, u32[]{:S(2)}) copy-start(s32[2]{0:T(128)} %gather_fusion) | copy-start | bytes 28
  76.3 14.4 %collective-permute-start.14 = (f32[2,2,128,256]{3,2,1,0:T(8,128)}, f32[2,2,128,256]{3,2,1,0:T(8,128)S(1)}, u32[]{:S(2)}, u32[]{:S(2)}) collective-permute-start(f32[2,2,128,256]{3,2,1,0:T(8,128)} %get-tuple-element.29), channel_id=1, source_target_pairs={{16,1},{17,0},{18,3},{19,2},{20,5},{21,4},{22,7},{23,6},{24,9},{25... | collective-permute-start | bytes 1572872 | tf_op jit(solution)/shard_map/ppermute | solution.py:311
  77.6 15.2 %collective-permute-start.12 = (f32[2,2,128,256]{3,2,1,0:T(8,128)}, f32[2,2,128,256]{3,2,1,0:T(8,128)S(1)}, u32[]{:S(2)}, u32[]{:S(2)}) collective-permute-start(f32[2,2,128,256]{3,2,1,0:T(8,128)} %get-tuple-element.29), channel_id=1, source_target_pairs={{0,1},{1,0},{2,3},{3,2},{4,5},{5,4},{6,7},{7,6},{8,9},{9,8},{10,11... | collective-permute-start | bytes 1572872 | tf_op jit(solution)/shard_map/ppermute | solution.py:311
  79.5 14.8 %collective-permute-start.20 = (f32[2,2,128,256]{3,2,1,0:T(8,128)}, f32[2,2,128,256]{3,2,1,0:T(8,128)S(1)}, u32[]{:S(2)}, u32[]{:S(2)}) collective-permute-start(f32[2,2,128,256]{3,2,1,0:T(8,128)} %get-tuple-element.31.refs_4_), channel_id=1, source_target_pairs={{19,1},{21,3},{23,5},{25,7},{27,9},{29,11},{31,13},{16,2},{18,4},{... | collective-permute-start | bytes 1572872 | tf_op jit(solution)/shard_map/ppermute | solution.py:311
  80.2 18.4 %collective-permute-start.18 = (f32[2,2,128,256]{3,2,1,0:T(8,128)}, f32[2,2,128,256]{3,2,1,0:T(8,128)S(1)}, u32[]{:S(2)}, u32[]{:S(2)}) collective-permute-start(f32[2,2,128,256]{3,2,1,0:T(8,128)} %get-tuple-element.31.refs_4_), channel_id=1, source_target_pairs={{3,1},{5,3},{7,5},{9,7},{11,9},{13,11},{15,13},{0,2},{2,4},{4,6},{... | collective-permute-start | bytes 1572872 | tf_op jit(solution)/shard_map/ppermute | solution.py:311
  85.4 14.8 %collective-permute-start.16 = (f32[2,2,128,256]{3,2,1,0:T(8,128)}, f32[2,2,128,256]{3,2,1,0:T(8,128)}, u32[]{:S(2)}, u32[]{:S(2)}) collective-permute-start(f32[2,2,128,256]{3,2,1,0:T(8,128)} %get-tuple-element.31.refs_4_), channel_id=1, source_target_pairs={{16,0},{17,1},{18,2},{19,3},{20,4},{21,5},{22,6},{23,7},{24,8},{25... | collective-permute-start | bytes 1572872 | tf_op jit(solution)/shard_map/ppermute | solution.py:311
  90.8 21.6 %copy-start.3 = (f32[2,2,128,256]{3,2,1,0:T(8,128)}, f32[2,2,128,256]{3,2,1,0:T(8,128)S(1)}, u32[]{:S(2)}) copy-start(f32[2,2,128,256]{3,2,1,0:T(8,128)S(1)} %collective-permute-done.14.refs_2_) | copy-start | bytes 1572868
  90.8 21.5 %collective-permute-start.15 = (f32[2,2,128,256]{3,2,1,0:T(8,128)}, f32[2,2,128,256]{3,2,1,0:T(8,128)}, u32[]{:S(2)}, u32[]{:S(2)}) collective-permute-start(f32[2,2,128,256]{3,2,1,0:T(8,128)} %get-tuple-element.30), channel_id=1, source_target_pairs={{0,17},{1,16},{2,19},{3,18},{4,21},{5,20},{6,23},{7,22},{8,25},{9,... | collective-permute-start | bytes 1572872 | tf_op jit(solution)/shard_map/ppermute | solution.py:311
  92.9 19.5 %copy-start.4 = (f32[2,2,128,256]{3,2,1,0:T(8,128)}, f32[2,2,128,256]{3,2,1,0:T(8,128)S(1)}, u32[]{:S(2)}) copy-start(f32[2,2,128,256]{3,2,1,0:T(8,128)S(1)} %collective-permute-done.12.refs_0_) | copy-start | bytes 1572868
  92.9 19.4 %collective-permute-start.13 = (f32[2,2,128,256]{3,2,1,0:T(8,128)}, f32[2,2,128,256]{3,2,1,0:T(8,128)}, u32[]{:S(2)}, u32[]{:S(2)}) collective-permute-start(f32[2,2,128,256]{3,2,1,0:T(8,128)} %get-tuple-element.30), channel_id=1, source_target_pairs={{16,17},{17,16},{18,19},{19,18},{20,21},{21,20},{22,23},{23,22},{2... | collective-permute-start | bytes 1572872 | tf_op jit(solution)/shard_map/ppermute | solution.py:311
  94.3 18.0 %copy-start.5 = (f32[2,2,128,256]{3,2,1,0:T(8,128)}, f32[2,2,128,256]{3,2,1,0:T(8,128)S(1)}, u32[]{:S(2)}) copy-start(f32[2,2,128,256]{3,2,1,0:T(8,128)S(1)} %collective-permute-done.20.refs_10_) | copy-start | bytes 1572868
  94.3 18.0 %collective-permute-start.21 = (f32[2,2,128,256]{3,2,1,0:T(8,128)S(1)}, f32[2,2,128,256]{3,2,1,0:T(8,128)}, u32[]{:S(2)}, u32[]{:S(2)}) collective-permute-start(f32[2,2,128,256]{3,2,1,0:T(8,128)S(1)} %copy-done.2), channel_id=1, source_target_pairs={{3,17},{5,19},{7,21},{9,23},{11,25},{13,27},{15,29},{0,18},{2,20},... | collective-permute-start | bytes 1572872 | tf_op jit(solution)/shard_map/ppermute | solution.py:311
  98.7 13.7 %copy-start.6 = (f32[2,2,128,256]{3,2,1,0:T(8,128)}, f32[2,2,128,256]{3,2,1,0:T(8,128)S(1)}, u32[]{:S(2)}) copy-start(f32[2,2,128,256]{3,2,1,0:T(8,128)S(1)} %collective-permute-done.18.refs_8_) | copy-start | bytes 1572868
  98.7 13.6 %collective-permute-start.19 = (f32[2,2,128,256]{3,2,1,0:T(8,128)S(1)}, f32[2,2,128,256]{3,2,1,0:T(8,128)}, u32[]{:S(2)}, u32[]{:S(2)}) collective-permute-start(f32[2,2,128,256]{3,2,1,0:T(8,128)S(1)} %copy-done.2), channel_id=1, source_target_pairs={{19,17},{21,19},{23,21},{25,23},{27,25},{29,27},{31,29},{16,18},{1... | collective-permute-start | bytes 1572872 | tf_op jit(solution)/shard_map/ppermute | solution.py:311
  100.1 12.2 %collective-permute-start.17 = (f32[2,2,128,256]{3,2,1,0:T(8,128)S(1)}, f32[2,2,128,256]{3,2,1,0:T(8,128)}, u32[]{:S(2)}, u32[]{:S(2)}) collective-permute-start(f32[2,2,128,256]{3,2,1,0:T(8,128)S(1)} %copy-done.2), channel_id=1, source_target_pairs={{0,16},{1,17},{2,18},{3,19},{4,20},{5,21},{6,22},{7,23},{8,24},{9,... | collective-permute-start | bytes 1572872 | tf_op jit(solution)/shard_map/ppermute | solution.py:311
where the time goes:
time: 118 us; the launch traced here: 117 us
  starting transfers between devices  43.4 us (37%)
  Pallas kernels  37.9 us (32%)
  local copies, waits for them, and re-layouts  14.6 us (12%)
  waiting for transfers between devices  13.5 us (11%)
  matrix products  4.01 us (3%)
  other arithmetic  3.48 us (3%)
    ppermute x19, starting transfers between devices, send(): lax.ppermute(value, AXES, [(a * tiles + s, b * tiles + t) for a, b in hop...  36.7 us
    ppermute x19, waiting for transfers between devices, send(): lax.ppermute(value, AXES, [(a * tiles + s, b * tiles + t) for a, b in hop...  13.5 us
    pallas_call x2, Pallas kernels, extract(): pl.pallas_call(functools.partial(extract_kernel, count), out_shape=[jax.S...  9.7 us
    pallas_call x1, Pallas kernels, local(): pl.pallas_call(second_kernel, out_shape=[band, band, pair], in_specs=[SME...  9.52 us
    pallas_call x1, Pallas kernels, local(): pl.pallas_call(first_kernel, out_shape=[slab, slab, pair], in_specs=[SMEM...  7.31 us
    another operation x1, local copies, waits for them, and re-layouts, local(): jnp.stack([depth, parity] + [own_cols[0], zero, own_cols[1], zero] + [par...  6.96 us
    pallas_call x1, Pallas kernels, local(): pl.pallas_call(third_kernel, out_shape=[band, band], in_specs=[VMEM] * 6,...  6.54 us
    ppermute x1, starting transfers between devices, local(): partner = lax.ppermute(scan_offsets, 'tile', swap)  5.77 us
  transfers between devices with their start and end apart: 22, of which 4 were waited for; matrix products, arithmetic and copies ran while one was open for 19% of the time, Pallas kernels for 15%

commit v1 on v0

v1 whole, which is shorter than its diff:
```python
import functools

import jax
import jax.numpy as jnp
import numpy as np
from jax import lax
from jax.experimental import pallas as pl
from jax.experimental.pallas import tpu as pltpu
from jax.sharding import PartitionSpec as P


F32 = jnp.float32
BF16 = jnp.bfloat16
AXES = ("depth", "tile")
ANY = pl.BlockSpec(memory_space=pl.ANY)
VMEM = pl.BlockSpec(memory_space=pltpu.VMEM)
HBM = pl.BlockSpec(memory_space=pltpu.HBM)
SMEM = pl.BlockSpec(memory_space=pltpu.SMEM)
cat = jnp.concatenate


def limit(mebibytes):
    return pltpu.CompilerParams(vmem_limit_bytes=mebibytes << 20)


def dft_tables(extent):
    half = extent // 2
    row, col = np.arange(half)[:, None], np.arange(half)[None, :]
    blocks = []
    for parity in (0, 1):
        turn = (row * (2 * col + parity)) % extent
        wave = np.exp(-2j * np.pi * turn / extent) / np.sqrt(extent)
        blocks.append(np.block([[wave.real, wave.imag], [-wave.imag, wave.real]]))
    table = np.stack([blocks[0], blocks[1], blocks[0].T, blocks[1].T])
    high = table.astype(np.float32).astype(BF16)
    low = (table - high.astype(np.float64)).astype(np.float32).astype(BF16)
    return np.stack([high, low], 1)


def split(x):
    high = x.astype(BF16)
    return high, (x - high.astype(F32)).astype(BF16)


def dot(a, b):
    return jnp.dot(a, b, preferred_element_type=F32)


def rmul(x, table, which):
    high, low = split(x)
    t_high, t_low = table[which, 0], table[which, 1]
    return dot(high, t_high) + (dot(low, t_high) + dot(high, t_low))


def lmul(table, which, x):
    high, low = split(x)
    t_high, t_low = table[which, 0], table[which, 1]
    return dot(t_high, high) + (dot(t_high, low) + dot(t_low, high))


def forward(xr, xi, table):
    h = xr.shape[0] // 2
    e = rmul(cat([xr[:, :h] + xr[:, h:], xi[:, :h] + xi[:, h:]], 1), table, 0)
    o = rmul(cat([xr[:, :h] - xr[:, h:], xi[:, :h] - xi[:, h:]], 1), table, 1)
    yr, yi = cat([e[:, :h], o[:, :h]], 1), cat([e[:, h:], o[:, h:]], 1)
    e = lmul(table, 2, cat([yr[:h] + yr[h:], yi[:h] + yi[h:]], 0))
    o = lmul(table, 3, cat([yr[:h] - yr[h:], yi[:h] - yi[h:]], 0))
    return cat([e[:h], o[:h]], 0), cat([e[h:], o[h:]], 0)


def inverse(xr, xi, table):
    h = xr.shape[0] // 2
    e = lmul(table, 0, cat([xr[:h], xi[:h]], 0))
    o = lmul(table, 1, cat([xr[h:], xi[h:]], 0))
    yr = cat([e[:h] + o[:h], e[:h] - o[:h]], 0)
    yi = cat([e[h:] + o[h:], e[h:] - o[h:]], 0)
    e = rmul(cat([yr[:, :h], yi[:, :h]], 1), table, 2)
    o = rmul(cat([yr[:, h:], yi[:, h:]], 1), table, 3)
    return (
        cat([e[:, :h] + o[:, :h], e[:, :h] - o[:, :h]], 1),
        cat([e[:, h:] + o[:, h:], e[:, h:] - o[:, h:]], 1),
    )


def times(ref, a, b, conj):
    pr, pi = ref[0], ref[1]
    if conj:
        return pr * a + pi * b, pr * b - pi * a
    return pr * a - pi * b, pr * b + pi * a


def place(column, patch, width):
    block = jnp.minimum(column // patch, width // patch - 2)
    return pl.multiple_of(block * patch, patch), column - block * patch


def extract_kernel(count, *refs):
    offsets, specimen = refs[:count], refs[count]
    outs, (wide, sems) = refs[count + 1 : 3 * count + 1], refs[3 * count + 1 :]
    depth = lax.axis_index("depth")
    layers, parts, rows = specimen.shape[:3]
    patch = outs[0].shape[3]
    shifts, copies = [], []
    for i in range(2 * count):
        position = depth if i % 2 == 0 else 1 - depth
        start, shift = place(offsets[i // 2][position, 1], patch, specimen.shape[3])
        shifts.append(shift)
        for s in range(layers):
            copy = pltpu.make_async_copy(
                specimen.at[s, :, :, pl.ds(start, 2 * patch)], wide.at[i, s], sems.at[i, s]
            )
            copy.start()
            copies.append(copy)
    lane = lax.broadcasted_iota(jnp.int32, (rows, patch), 1)
    for i in range(2 * count):
        for s in range(layers):
            copies[i * layers + s].wait()
            for c in range(parts):
                outs[i][s, c] = jnp.where(
                    lane < shifts[i], wide[i, s, c, :, patch:], wide[i, s, c, :, :patch]
                )


def extract(specimen, offsets, patch):
    count = len(offsets)
    layers, parts, rows, _ = specimen.shape
    size = 2 * count * layers * parts * rows * patch
    return pl.pallas_call(
        functools.partial(extract_kernel, count),
        out_shape=[jax.ShapeDtypeStruct((layers, parts, rows, patch), F32)] * (2 * count),
        in_specs=[SMEM] * count + [HBM],
        out_specs=[VMEM] * (2 * count),
        scratch_shapes=[
            pltpu.VMEM((2 * count, layers, parts, rows, 2 * patch), F32),
            pltpu.SemaphoreType.DMA((2 * count, layers)),
        ],
        cost_estimate=pl.CostEstimate(flops=size, bytes_accessed=12 * size, transcendentals=0),
        compiler_params=limit(16),
        name="extract",
    )(*offsets, pltpu.with_memory_space_constraint(specimen, pltpu.HBM))


def top_row(offsets, position, holder, rows):
    return offsets[position, 0] - (holder - 1) * rows


def work_kernel(core, offsets, probe, kernel, table, target, *refs):
    mids, fars, nears, refs = refs[0:2], refs[2:4], refs[4:6], refs[6:]
    tops, lows, (patches, waves, cur, third, own, sems) = refs[0:2], refs[2:4], refs[4:]
    count = patches.shape[0]
    layers, parts, rows, patch = third.shape[1:]
    groups = (core, 1 - core)

    @pl.when(lax.axis_index("depth") == core)
    def _():
        tile = lax.axis_index("tile")
        copies = []
        for i, group in enumerate(groups):
            part = patches.at[pl.ds(group * layers, layers), :, pl.ds(rows, rows), :]
            copies += [
                pltpu.make_async_copy(mids[i], part, sems.at[i, 0]),
                pltpu.make_async_copy(fars[i], third.at[group], sems.at[i, 1]),
                pltpu.make_async_copy(nears[i], own.at[group], sems.at[i, 2]),
            ]
        for copy in copies:
            copy.start()
        down = top_row(offsets, core, tile ^ 1, rows)
        right = offsets[core, 1] % patch
        for c in range(2):
            waves[0, c] = pltpu.roll(pltpu.roll(probe[c], down, 0), right, 1)
        row = lax.broadcasted_iota(jnp.int32, (rows, patch), 0)
        from_own = (row < down) == (tile % 2 == 1)
        for copy in copies:
            copy.wait()
        for s in range(count):
            for c in range(parts):
                g, r = divmod(s, layers)
                patches[s, c, :rows] = jnp.where(from_own, own[g, r, c], third[g, r, c])
        cur[0], cur[1] = times(patches.at[0], waves[0, 0], waves[0, 1], False)

        def step(s, unused):
            a, b = forward(cur[0], cur[1], table)
            exit_step = s == count - 1
            residue = 2.0 * (a * a + b * b - target[...])
            kr = jnp.where(exit_step, residue, kernel[0])
            ki = jnp.where(exit_step, 0.0, jnp.where(s < count, kernel[1], -kernel[1]))
            a, b = kr * a - ki * b, kr * b + ki * a
            cur[0], cur[1] = inverse(a, b, table)

            @pl.when(s < count - 1)
            def _():
                waves[s + 1] = cur[...]
                cur[0], cur[1] = times(patches.at[s + 1], cur[0], cur[1], False)

            @pl.when(s >= count - 1)
            def _():
                k = 2 * (count - 1) - s
                a, b = times(waves.at[k], cur[0], cur[1], True)
                for i, group in enumerate(groups):

                    @pl.when(k // layers == group)
                    def _():
                        r = k % layers
                        tops[i][r, 0], tops[i][r, 1] = a[:rows], b[:rows]
                        lows[i][r, 0], lows[i][r, 1] = a[rows:], b[rows:]

                cur[0], cur[1] = times(patches.at[k], cur[0], cur[1], True)

            return unused

        lax.fori_loop(0, 2 * count - 1, step, 0)


def work(core, offsets, probe, kernel, table, target, *sources):
    layers, parts, rows, patch = sources[0].shape
    band = jax.ShapeDtypeStruct(sources[0].shape, F32)
    full_v = pltpu.VMEM((2 * layers, parts, patch, patch), F32)
    band_v = pltpu.VMEM((2, layers, parts, rows, patch), F32)
    flops = 28 * layers * 12 * patch**3
    return pl.pallas_call(
        functools.partial(work_kernel, core),
        out_shape=[band] * 4,
        in_specs=[SMEM] + [VMEM] * 4 + [ANY] * 6,
        out_specs=[VMEM] * 4,
        scratch_shapes=[
            full_v,
            full_v,
            pltpu.VMEM((parts, patch, patch), F32),
            band_v,
            band_v,
            pltpu.SemaphoreType.DMA((2, 3)),
        ],
        cost_estimate=pl.CostEstimate(flops=flops, bytes_accessed=8 << 20, transcendentals=0),
        compiler_params=limit(28),
        name="work",
    )(offsets, probe, kernel, table, target, *sources)


def pick(depth, at_zero, at_one, dst, sem):
    @pl.when(depth == 0)
    def _():
        pltpu.make_async_copy(at_zero, dst, sem).start()

    @pl.when(depth != 0)
    def _():
        pltpu.make_async_copy(at_one, dst, sem).start()

    return pltpu.make_async_copy(at_zero, dst, sem)


def gather_kernel(own, partner, their, *refs):
    sources, (out, windows, total, sems, out_sems) = refs[:12], refs[12:]
    layers, parts, rows, patch = windows.shape[1:]
    depth, tile = lax.axis_index("depth"), lax.axis_index("tile")
    copies = [
        pick(depth, sources[2 * i], sources[2 * i + 1], windows.at[i], sems.at[i])
        for i in range(6)
    ]
    row = lax.broadcasted_iota(jnp.int32, (rows, patch), 0)
    lane = lax.broadcasted_iota(jnp.int32, (rows, patch), 1)
    odd = tile % 2 == 1
    total[...] = jnp.zeros_like(total)
    facts = []
    for i in range(6):
        offsets = (own, partner, their)[i // 2]
        position = depth if i % 2 == 0 else 1 - depth
        holder = (tile, tile ^ 1, jnp.where(odd, tile + 1, tile - 1))[i // 2]
        start, shift = place(offsets[position, 1], patch, total.shape[3])
        facts.append((start, shift, top_row(offsets, position, holder, rows)))
    for copy in copies:
        copy.wait()
    sends = []
    for s in range(layers):
        for c in range(parts):
            for i in range(6):
                start, shift, down = facts[i]
                value = windows[i, s, c]
                if i >= 2:
                    above = row < down
                    keep = (above == odd) if i < 4 else (above != odd)
                    value = jnp.where(keep, value, 0.0)
                near = pl.ds(start, patch)
                far = pl.ds(pl.multiple_of(start + patch, patch), patch)
                total[s, c, :, near] += jnp.where(lane < shift, 0.0, value)
                total[s, c, :, far] += jnp.where(lane < shift, value, 0.0)
            copy = pltpu.make_async_copy(total.at[s, c], out.at[s, c], out_sems.at[s, c])
            copy.start()
            sends.append(copy)
    for copy in sends:
        copy.wait()


def local(specimen, scan_offsets, probe_wave, fresnel_phase, measured):
    layers, parts, rows, width = specimen.shape
    patch = probe_wave.shape[-1]
    tiles, depths = lax.axis_size("tile"), lax.axis_size("depth")
    assert depths == 2 and scan_offsets.shape[0] == depths
    assert tiles % 2 == 0 and patch == 2 * rows and width % patch == 0
    depth = lax.axis_index("depth")

    swap = [(t, t ^ 1) for t in range(tiles)]
    other = [(t, t + 1) for t in range(1, tiles - 1, 2)] + [(t, t - 1) for t in range(2, tiles, 2)]
    outward = [(t, t + 2) for t in range(1, tiles - 2, 2)] + [
        (t, t - 2) for t in range(2, tiles, 2)
    ]
    homeward = [(b, a) for a, b in outward]
    stay = [(t, t) for t in range(tiles)]
    same, cross = [(0, 0), (1, 1)], [(0, 1), (1, 0)]

    def send(value, pairs, hops):
        return lax.ppermute(
            value, AXES, [(a * tiles + s, b * tiles + t) for a, b in hops for s, t in pairs]
        )

    their = send(scan_offsets, other, same)
    target = lax.dynamic_index_in_dim(measured, depth, 0, keepdims=False)
    target = send(target, swap, same)
    partner = send(scan_offsets, swap, same)

    table = jnp.asarray(dft_tables(patch))
    places = np.concatenate([np.arange(0, patch, 2), np.arange(1, patch, 2)])
    pick_one = jnp.asarray(np.eye(patch, dtype=np.float32)[places])

    def reorder(x):
        x = jnp.dot(pick_one, x, precision=lax.Precision.HIGHEST)
        return jnp.dot(x, pick_one.T, precision=lax.Precision.HIGHEST)

    phase = reorder(fresnel_phase)
    kernel = jnp.stack([jnp.cos(phase), jnp.sin(phase)], 0)
    their, kernel = lax.optimization_barrier((their, kernel))
    found = extract(specimen, [their, scan_offsets, partner], patch)
    far, mid, near = found[0:2], found[2:4], found[4:6]
    mids, fars = [], []
    for core in range(2):
        for step in range(2):
            hop = [((core + step) % 2, core)]
            mids.append(send(mid[step], swap, hop))
            fars.append(send(far[step], outward, hop))
    near_other = send(near[1], stay, cross)
    target = reorder(target)

    kept, others, lows, tops = [], [], [], []
    for core in range(2):
        grads = work(
            core, partner, probe_wave, kernel, table, target,
            *mids[2 * core : 2 * core + 2], *fars[2 * core : 2 * core + 2],
            near[0], near_other,
        )
        for step in range(2):
            hop = [(core, (core + step) % 2)]
            tops.append(send(grads[step], homeward, hop))
            lows.append(send(grads[2 + step], swap, hop))
        kept.append(grads[0])
        others.append(send(grads[1], stay, [(core, 1 - core)]))
    windows = [lows[0], lows[2], lows[3], lows[1]]
    windows += [kept[0], kept[1], others[1], others[0]]
    windows += [tops[0], tops[2], tops[3], tops[1]]
    return pl.pallas_call(
        gather_kernel,
        out_shape=jax.ShapeDtypeStruct(specimen.shape, F32),
        in_specs=[SMEM] * 3 + [ANY] * 12,
        out_specs=ANY,
        scratch_shapes=[
            pltpu.VMEM((6, layers, parts, rows, patch), F32),
            pltpu.VMEM(specimen.shape, F32),
            pltpu.SemaphoreType.DMA((6,)),
            pltpu.SemaphoreType.DMA((layers, parts)),
        ],
        cost_estimate=pl.CostEstimate(flops=6 << 20, bytes_accessed=7 << 20, transcendentals=0),
        compiler_params=limit(16),
        name="gather",
    )(scan_offsets, partner, their, *windows)


def solution(mesh):
    placed = (P("depth", None, "tile", None), P("tile", None), P(), P(), P("tile", None, None))

    return jax.shard_map(
        local,
        mesh=mesh,
        in_specs=placed,
        out_specs=P("depth", None, "tile", None),
        check_vma=False,
    )
```

time: 118 us -> 94.9 us (0.80)
  the two profiles are of different devices: /device:TPU:0 before, /device:TPU:25 now
where the time goes in v1:
time: 94.9 us; the launch traced here: 94.4 us
  starting transfers between devices  37.3 us (39%)
  waiting for transfers between devices  29.4 us (31%)
  Pallas kernels  21.4 us (23%)
  matrix products  5.13 us (5%)
    ppermute x22, starting transfers between devices, send(): lax.ppermute(value, AXES, [(a * tiles + s, b * tiles + t) for a, b in hop...  37.3 us
    ppermute x22, waiting for transfers between devices, send(): lax.ppermute(value, AXES, [(a * tiles + s, b * tiles + t) for a, b in hop...  29.4 us
    pallas_call x2, Pallas kernels, work(): pl.pallas_call(functools.partial(work_kernel, core), out_shape=[band] * 4...  14.2 us
    pallas_call x1, Pallas kernels, extract(): pl.pallas_call(functools.partial(extract_kernel, count), out_shape=[jax.S...  3.73 us
    pallas_call x1, Pallas kernels, local(): pl.pallas_call(gather_kernel, out_shape=jax.ShapeDtypeStruct(specimen.sha...  3.44 us
    dot_general x2, matrix products, reorder(): return jnp.dot(x, pick_one.T, precision=lax.Precision.HIGHEST)  3.12 us
    dot_general x2, matrix products, reorder(): x = jnp.dot(pick_one, x, precision=lax.Precision.HIGHEST)  2.01 us
  transfers between devices with their start and end apart: 22, of which 5 were waited for; matrix products, arithmetic and copies ran while one was open for 5% of the time, Pallas kernels for 19%

profile of v1, /device:TPU:25, one launch (start us, length us, event | category | flops | bytes accessed | tf_op | source)
XLA Modules:
  0.0 94.4 jit_solution(17646573199579029076)
XLA Ops:
  0.0 4.1 %collective-permute-start.1 = (s32[2,2]{1,0:T(2,128)}, s32[2,2]{1,0:T(2,128)S(1)}, u32[]{:S(2)}, u32[]{:S(2)}) collective-permute-start(s32[2,2]{1,0:T(2,128)} %own.1), channel_id=1, source_target_pairs={{1,2},{3,4},{5,6},{7,8},{9,10},{11,12},{13,14},{2,1},{4,3},{6,5},{... | collective-permute-start | bytes 56 | tf_op jit(solution)/shard_map/ppermute | solution.py:311
  4.1 0.4 collective-permute-start
  4.6 0.0 copy-start.3
  4.6 0.0 copy-start.4
  4.6 1.2 %collective-permute-start.2 = (f32[256,256]{1,0:T(8,128)S(1)}, f32[256,256]{1,0:T(8,128)S(1)}, u32[]{:S(2)}, u32[]{:S(2)}) collective-permute-start(f32[256,256]{1,0:T(8,128)S(1)} %dynamic-slice_bitcast_fusion), channel_id=1, source_target_pairs={{0,1},{1,0},{2,3},{3,2},{4,5},{5,4},{6,7},{7,6},{8,9},{9,8},{10,11... | collective-permute-start | bytes 786440 | tf_op jit(solution)/shard_map/ppermute | solution.py:311
  5.7 1.4 %fusion = f32[256,256]{1,0:T(8,128)S(1)} fusion(f32[256,256]{1,0:T(8,128)} %constant.17.clone, f32[256,256]{1,0:T(8,128)} %param.10), kind=kOutput, calls=%fused_computation.4 | convolution fusion | flops 201326592 | bytes 786432 | tf_op jit(solution)/shard_map/dot_general | solution.py:325
  7.2 2.5 %cosine_bitcast_fusion = (f32[1,256,256]{2,1,0:T(8,128)S(1)}, f32[1,256,256]{2,1,0:T(8,128)S(1)}) fusion(f32[256,256]{1,0:T(8,128)S(1)} %fusion, f32[256,256]{1,0:T(8,128)} %constant.17.clone), kind=kOutput, calls=%fused_computation.3 | convolution fusion | flops 201326592 | bytes 1048576 | tf_op jit(solution)/shard_map/dot_general | solution.py:326
  9.7 0.0 collective-permute-done.1.refs_0_.their
  9.8 0.0 copy-start.1
  9.8 0.7 copy-done.1
  10.4 3.7 %extract.1 = (f32[2,2,128,256]{3,2,1,0:T(8,128)S(1)}, f32[2,2,128,256]{3,2,1,0:T(8,128)S(1)}, f32[2,2,128,256]{3,2,1,0:T(8,128)S(1)}, f32[2,2,128,256]{3,2,1,0:T...) custom-call(s32[2,2]{1,0:T(2,128)S(1)} %collective-permute-done.1.refs_0_.their, ...), custom_call_target="tpu_custom_call" | custom-call | flops 786432 | bytes 9437184 | tf_op jit(solution)/shard_map/extract/pallas_call | solution.py:128
  14.2 1.6 %collective-permute-start.7 = (f32[2,2,128,256]{3,2,1,0:T(8,128)S(1)}, f32[2,2,128,256]{3,2,1,0:T(8,128)S(1)}, u32[]{:S(2)}, u32[]{:S(2)}) collective-permute-start(f32[2,2,128,256]{3,2,1,0:T(8,128)S(1)} %get-tuple-element.28), channel_id=1, source_target_pairs={{0,16},{1,17},{2,18},{3,19},{4,20},{5,21},{6,22},{7,23},{8,24},{9,... | collective-permute-start | bytes 1572872 | tf_op jit(solution)/shard_map/ppermute | solution.py:311
  15.8 2.1 %collective-permute-start.9 = (f32[2,2,128,256]{3,2,1,0:T(8,128)S(1)}, f32[2,2,128,256]{3,2,1,0:T(8,128)S(1)}, u32[]{:S(2)}, u32[]{:S(2)}) collective-permute-start(f32[2,2,128,256]{3,2,1,0:T(8,128)S(1)} %get-tuple-element.23), channel_id=1, source_target_pairs={{16,17},{17,16},{18,19},{19,18},{20,21},{21,20},{22,23},{23,22},{2... | collective-permute-start | bytes 1572872 | tf_op jit(solution)/shard_map/ppermute | solution.py:311
  17.8 1.3 %collective-permute-start.10 = (f32[2,2,128,256]{3,2,1,0:T(8,128)S(1)}, f32[2,2,128,256]{3,2,1,0:T(8,128)S(1)}, u32[]{:S(2)}, u32[]{:S(2)}) collective-permute-start(f32[2,2,128,256]{3,2,1,0:T(8,128)S(1)} %get-tuple-element.24), channel_id=1, source_target_pairs={{0,17},{1,16},{2,19},{3,18},{4,21},{5,20},{6,23},{7,22},{8,25},{9,... | collective-permute-start | bytes 1572872 | tf_op jit(solution)/shard_map/ppermute | solution.py:311
  19.1 3.0 %collective-permute-start.11 = (f32[2,2,128,256]{3,2,1,0:T(8,128)S(1)}, f32[2,2,128,256]{3,2,1,0:T(8,128)S(1)}, u32[]{:S(2)}, u32[]{:S(2)}) collective-permute-start(f32[2,2,128,256]{3,2,1,0:T(8,128)S(1)} %get-tuple-element.25), channel_id=1, source_target_pairs={{17,19},{19,21},{21,23},{23,25},{25,27},{27,29},{29,31},{18,16},{2... | collective-permute-start | bytes 1572872 | tf_op jit(solution)/shard_map/ppermute | solution.py:311
  22.2 0.0 collective-permute-done.2
  22.2 1.3 %collective-permute-start.12 = (f32[2,2,128,256]{3,2,1,0:T(8,128)S(1)}, f32[2,2,128,256]{3,2,1,0:T(8,128)S(1)}, u32[]{:S(2)}, u32[]{:S(2)}) collective-permute-start(f32[2,2,128,256]{3,2,1,0:T(8,128)S(1)} %get-tuple-element.26), channel_id=1, source_target_pairs={{1,19},{3,21},{5,23},{7,25},{9,27},{11,29},{13,31},{2,16},{4,18},{... | collective-permute-start | bytes 1572872 | tf_op jit(solution)/shard_map/ppermute | solution.py:311
  23.5 0.6 fusion.1
  24.1 0.6 fusion.2.target
  24.7 0.0 collective-permute-done.7.refs_5_
  24.7 0.7 collective-permute-start.3
  25.4 3.2 %collective-permute-done.9.refs_0_ = f32[2,2,128,256]{3,2,1,0:T(8,128)S(1)} collective-permute-done((f32[2,2,128,256]{3,2,1,0:T(8,128)S(1)}, f32[2,2,128,256]{3,2,1,0:T(8,128)S(1)}, u32[]{:S(2)}, u32[]{:S(2)}) %collective-permute-start.9) | collective-permute-done | bytes 524320 | tf_op jit(solution)/shard_map/ppermute | solution.py:311
  28.6 3.1 %collective-permute-start.4 = (f32[2,2,128,256]{3,2,1,0:T(8,128)S(1)}, f32[2,2,128,256]{3,2,1,0:T(8,128)S(1)}, u32[]{:S(2)}, u32[]{:S(2)}) collective-permute-start(f32[2,2,128,256]{3,2,1,0:T(8,128)S(1)} %get-tuple-element.24), channel_id=1, source_target_pairs={{16,1},{17,0},{18,3},{19,2},{20,5},{21,4},{22,7},{23,6},{24,9},{25... | collective-permute-start | bytes 1572872 | tf_op jit(solution)/shard_map/ppermute | solution.py:311
  31.7 0.0 collective-permute-done.10.refs_1_
  31.7 0.7 collective-permute-start.5
  32.4 4.9 %collective-permute-start.6 = (f32[2,2,128,256]{3,2,1,0:T(8,128)S(1)}, f32[2,2,128,256]{3,2,1,0:T(8,128)S(1)}, u32[]{:S(2)}, u32[]{:S(2)}) collective-permute-start(f32[2,2,128,256]{3,2,1,0:T(8,128)S(1)} %get-tuple-element.26), channel_id=1, source_target_pairs={{17,3},{19,5},{21,7},{23,9},{25,11},{27,13},{29,15},{18,0},{20,2},... | collective-permute-start | bytes 1572872 | tf_op jit(solution)/shard_map/ppermute | solution.py:311
  37.3 0.0 collective-permute-done.12.refs_3_
  37.3 13.6 %work.3 = (f32[2,2,128,256]{3,2,1,0:T(8,128)S(1)}, f32[2,2,128,256]{3,2,1,0:T(8,128)S(1)}, f32[2,2,128,256]{3,2,1,0:T(8,128)S(1)}, f32[2,2,128,256]{3,2,1,0:T(8,128)S(1)}) custom-call(s32[2,2]{1,0:T(2,128)S(1)} %collective-permute-done.refs_2_.offsets.partner, f32[2,256,256]{2,1,0:T(8,128)S(1)} %copy-done.3, f32[2,256,256]{2,1,0:T(8,128)S(1)} %pad_maximum_fusion.kernel, ...), custom_call_target="tpu_custom_call" | custom-call | flops 11274289152 | bytes 8388608 | tf_op jit(solution)/shard_map/work/pallas_call | solution.py:220
  51.0 1.3 %collective-permute-start.20 = (f32[2,2,128,256]{3,2,1,0:T(8,128)S(1)}, f32[2,2,128,256]{3,2,1,0:T(8,128)S(1)}, u32[]{:S(2)}, u32[]{:S(2)}) collective-permute-start(f32[2,2,128,256]{3,2,1,0:T(8,128)S(1)} %get-tuple-element.35), channel_id=1, source_target_pairs={{19,1},{21,3},{23,5},{25,7},{27,9},{29,11},{31,13},{16,2},{18,4},{... | collective-permute-start | bytes 1572872 | tf_op jit(solution)/shard_map/ppermute | solution.py:311
  52.3 1.3 %collective-permute-start.16 = (f32[2,2,128,256]{3,2,1,0:T(8,128)S(1)}, f32[2,2,128,256]{3,2,1,0:T(8,128)S(1)}, u32[]{:S(2)}, u32[]{:S(2)}) collective-permute-start(f32[2,2,128,256]{3,2,1,0:T(8,128)S(1)} %get-tuple-element.35), channel_id=1, source_target_pairs={{16,0},{17,1},{18,2},{19,3},{20,4},{21,5},{22,6},{23,7},{24,8},{25... | collective-permute-start | bytes 1572872 | tf_op jit(solution)/shard_map/ppermute | solution.py:311
  53.6 0.0 collective-permute-done.4.refs_1_
  53.7 1.9 %collective-permute-start.13 = (f32[2,2,128,256]{3,2,1,0:T(8,128)S(1)}, f32[2,2,128,256]{3,2,1,0:T(8,128)S(1)}, u32[]{:S(2)}, u32[]{:S(2)}) collective-permute-start(f32[2,2,128,256]{3,2,1,0:T(8,128)S(1)} %get-tuple-element.30), channel_id=1, source_target_pairs={{16,17},{17,16},{18,19},{19,18},{20,21},{21,20},{22,23},{23,22},{2... | collective-permute-start | bytes 1572872 | tf_op jit(solution)/shard_map/ppermute | solution.py:311
  55.6 1.3 %collective-permute-start.14 = (f32[2,2,128,256]{3,2,1,0:T(8,128)S(1)}, f32[2,2,128,256]{3,2,1,0:T(8,128)S(1)}, u32[]{:S(2)}, u32[]{:S(2)}) collective-permute-start(f32[2,2,128,256]{3,2,1,0:T(8,128)S(1)} %get-tuple-element.31), channel_id=1, source_target_pairs={{16,1},{17,0},{18,3},{19,2},{20,5},{21,4},{22,7},{23,6},{24,9},{25... | collective-permute-start | bytes 1572872 | tf_op jit(solution)/shard_map/ppermute | solution.py:311
  56.9 0.0 collective-permute-done.6.refs_3_
  56.9 0.0 copy-start.2
  56.9 1.9 %collective-permute-start.19 = (f32[2,2,128,256]{3,2,1,0:T(8,128)S(1)}, f32[2,2,128,256]{3,2,1,0:T(8,128)S(1)}, u32[]{:S(2)}, u32[]{:S(2)}) collective-permute-start(f32[2,2,128,256]{3,2,1,0:T(8,128)S(1)} %get-tuple-element.34.refs_5_), channel_id=1, source_target_pairs={{19,17},{21,19},{23,21},{25,23},{27,25},{29,27},{31,29},{16,18},{1... | collective-permute-start | bytes 1572872 | tf_op jit(solution)/shard_map/ppermute | solution.py:311
  58.9 0.6 work.2
  59.5 4.1 %collective-permute-done.13.refs_1_ = f32[2,2,128,256]{3,2,1,0:T(8,128)S(1)} collective-permute-done((f32[2,2,128,256]{3,2,1,0:T(8,128)S(1)}, f32[2,2,128,256]{3,2,1,0:T(8,128)S(1)}, u32[]{:S(2)}, u32[]{:S(2)}) %collective-permute-start.13) | collective-permute-done | bytes 524320 | tf_op jit(solution)/shard_map/ppermute | solution.py:311
  63.6 0.7 collective-permute-start.8
  64.3 4.2 %collective-permute-done.14.refs_2_ = f32[2,2,128,256]{3,2,1,0:T(8,128)S(1)} collective-permute-done((f32[2,2,128,256]{3,2,1,0:T(8,128)S(1)}, f32[2,2,128,256]{3,2,1,0:T(8,128)S(1)}, u32[]{:S(2)}, u32[]{:S(2)}) %collective-permute-start.14) | collective-permute-done | bytes 524320 | tf_op jit(solution)/shard_map/ppermute | solution.py:311
  68.5 1.3 %collective-permute-start.15 = (f32[2,2,128,256]{3,2,1,0:T(8,128)S(1)}, f32[2,2,128,256]{3,2,1,0:T(8,128)S(1)}, u32[]{:S(2)}, u32[]{:S(2)}) collective-permute-start(f32[2,2,128,256]{3,2,1,0:T(8,128)S(1)} %get-tuple-element.32), channel_id=1, source_target_pairs={{0,17},{1,16},{2,19},{3,18},{4,21},{5,20},{6,23},{7,22},{8,25},{9,... | collective-permute-start | bytes 1572872 | tf_op jit(solution)/shard_map/ppermute | solution.py:311
  69.7 0.0 collective-permute-done.19.refs_9_
  69.8 0.7 collective-permute-start.18
  70.5 1.3 %collective-permute-start.21 = (f32[2,2,128,256]{3,2,1,0:T(8,128)S(1)}, f32[2,2,128,256]{3,2,1,0:T(8,128)S(1)}, u32[]{:S(2)}, u32[]{:S(2)}) collective-permute-start(f32[2,2,128,256]{3,2,1,0:T(8,128)S(1)} %get-tuple-element.36), channel_id=1, source_target_pairs={{3,17},{5,19},{7,21},{9,23},{11,25},{13,27},{15,29},{0,18},{2,20},... | collective-permute-start | bytes 1572872 | tf_op jit(solution)/shard_map/ppermute | solution.py:311
  71.8 1.3 %collective-permute-start.17 = (f32[2,2,128,256]{3,2,1,0:T(8,128)S(1)}, f32[2,2,128,256]{3,2,1,0:T(8,128)S(1)}, u32[]{:S(2)}, u32[]{:S(2)}) collective-permute-start(f32[2,2,128,256]{3,2,1,0:T(8,128)S(1)} %get-tuple-element.36), channel_id=1, source_target_pairs={{0,16},{1,17},{2,18},{3,19},{4,20},{5,21},{6,22},{7,23},{8,24},{9,... | collective-permute-start | bytes 1572872 | tf_op jit(solution)/shard_map/ppermute | solution.py:311
  73.1 7.6 %collective-permute-done.15.refs_3_ = f32[2,2,128,256]{3,2,1,0:T(8,128)S(1)} collective-permute-done((f32[2,2,128,256]{3,2,1,0:T(8,128)S(1)}, f32[2,2,128,256]{3,2,1,0:T(8,128)S(1)}, u32[]{:S(2)}, u32[]{:S(2)}) %collective-permute-start.15) | collective-permute-done | bytes 524320 | tf_op jit(solution)/shard_map/ppermute | solution.py:311
  80.7 10.3 %collective-permute-done.21.refs_11_ = f32[2,2,128,256]{3,2,1,0:T(8,128)S(1)} collective-permute-done((f32[2,2,128,256]{3,2,1,0:T(8,128)S(1)}, f32[2,2,128,256]{3,2,1,0:T(8,128)S(1)}, u32[]{:S(2)}, u32[]{:S(2)}) %collective-permute-start.21) | collective-permute-done | bytes 524320 | tf_op jit(solution)/shard_map/ppermute | solution.py:311
  91.0 3.4 %gather.1 = f32[2,2,128,2048]{3,2,1,0:T(8,128)} custom-call(s32[2,2]{1,0:T(2,128)S(1)} %copy-done.2, s32[2,2]{1,0:T(2,128)S(1)} %collective-permute-done.refs_2_.offsets.partner, s32[2,2]{1,0:T(2,128)S(1)} %collective-permute-done.1.refs_0_.their, f32[2,2,128,256]{3,2,1,0:T(8,128)S(1)} %collective-permute-done.8.refs_0_, ...), custom_call_target="tpu_custom_call" | custom-call | flops 6291456 | bytes 7340032 | tf_op jit(solution)/shard_map/gather/pallas_call | solution.py:358
  (18 shorter events, 0.1 us)
Async XLA Ops:
  0.0 4.5 %copy-start = (f32[2,256,256]{2,1,0:T(8,128)S(1)}, f32[2,256,256]{2,1,0:T(8,128)}, u32[]{:S(2)}) copy-start(f32[2,256,256]{2,1,0:T(8,128)} %param.11) | copy-start | bytes 1572868
  0.0 23.5 %copy-start.5 = (f32[256,256]{1,0:T(8,128)S(1)}, f32[256,256]{1,0:T(8,128)}, u32[]{:S(2)}) copy-start(f32[256,256]{1,0:T(8,128)} %constant.17.clone) | copy-start | bytes 786436
  0.0 9.7 %collective-permute-start.1 = (s32[2,2]{1,0:T(2,128)}, s32[2,2]{1,0:T(2,128)S(1)}, u32[]{:S(2)}, u32[]{:S(2)}) collective-permute-start(s32[2,2]{1,0:T(2,128)} %own.1), channel_id=1, source_target_pairs={{1,2},{3,4},{5,6},{7,8},{9,10},{11,12},{13,14},{2,1},{4,3},{6,5},{... | collective-permute-start | bytes 56 | tf_op jit(solution)/shard_map/ppermute | solution.py:311
  4.1 5.6 %collective-permute-start = (s32[2,2]{1,0:T(2,128)}, s32[2,2]{1,0:T(2,128)S(1)}, u32[]{:S(2)}, u32[]{:S(2)}) collective-permute-start(s32[2,2]{1,0:T(2,128)} %own.1), channel_id=1, source_target_pairs={{0,1},{1,0},{2,3},{3,2},{4,5},{5,4},{6,7},{7,6},{8,9},{9,8},{10,11... | collective-permute-start | bytes 56 | tf_op jit(solution)/shard_map/ppermute | solution.py:311
  4.6 32.8 %copy-start.3 = (f32[2,256,256]{2,1,0:T(8,128)S(1)}, f32[2,256,256]{2,1,0:T(8,128)}, u32[]{:S(2)}) copy-start(f32[2,256,256]{2,1,0:T(8,128)} %probe.3) | copy-start | bytes 1572868
  4.6 32.8 %copy-start.4 = (bf16[4,2,256,256]{3,2,1,0:T(8,128)(2,1)S(1)}, bf16[4,2,256,256]{3,2,1,0:T(8,128)(2,1)}, u32[]{:S(2)}) copy-start(bf16[4,2,256,256]{3,2,1,0:T(8,128)(2,1)} %constant.16.clone.table) | copy-start | bytes 3145732
  4.6 17.6 %collective-permute-start.2 = (f32[256,256]{1,0:T(8,128)S(1)}, f32[256,256]{1,0:T(8,128)S(1)}, u32[]{:S(2)}, u32[]{:S(2)}) collective-permute-start(f32[256,256]{1,0:T(8,128)S(1)} %dynamic-slice_bitcast_fusion), channel_id=1, source_target_pairs={{0,1},{1,0},{2,3},{3,2},{4,5},{5,4},{6,7},{7,6},{8,9},{9,8},{10,11... | collective-permute-start | bytes 786440 | tf_op jit(solution)/shard_map/ppermute | solution.py:311
  9.8 0.7 copy-start.1
  14.2 10.6 %collective-permute-start.7 = (f32[2,2,128,256]{3,2,1,0:T(8,128)S(1)}, f32[2,2,128,256]{3,2,1,0:T(8,128)S(1)}, u32[]{:S(2)}, u32[]{:S(2)}) collective-permute-start(f32[2,2,128,256]{3,2,1,0:T(8,128)S(1)} %get-tuple-element.28), channel_id=1, source_target_pairs={{0,16},{1,17},{2,18},{3,19},{4,20},{5,21},{6,22},{7,23},{8,24},{9,... | collective-permute-start | bytes 1572872 | tf_op jit(solution)/shard_map/ppermute | solution.py:311
  15.8 12.9 %collective-permute-start.9 = (f32[2,2,128,256]{3,2,1,0:T(8,128)S(1)}, f32[2,2,128,256]{3,2,1,0:T(8,128)S(1)}, u32[]{:S(2)}, u32[]{:S(2)}) collective-permute-start(f32[2,2,128,256]{3,2,1,0:T(8,128)S(1)} %get-tuple-element.23), channel_id=1, source_target_pairs={{16,17},{17,16},{18,19},{19,18},{20,21},{21,20},{22,23},{23,22},{2... | collective-permute-start | bytes 1572872 | tf_op jit(solution)/shard_map/ppermute | solution.py:311
  17.8 13.9 %collective-permute-start.10 = (f32[2,2,128,256]{3,2,1,0:T(8,128)S(1)}, f32[2,2,128,256]{3,2,1,0:T(8,128)S(1)}, u32[]{:S(2)}, u32[]{:S(2)}) collective-permute-start(f32[2,2,128,256]{3,2,1,0:T(8,128)S(1)} %get-tuple-element.24), channel_id=1, source_target_pairs={{0,17},{1,16},{2,19},{3,18},{4,21},{5,20},{6,23},{7,22},{8,25},{9,... | collective-permute-start | bytes 1572872 | tf_op jit(solution)/shard_map/ppermute | solution.py:311
  19.1 13.3 %collective-permute-start.11 = (f32[2,2,128,256]{3,2,1,0:T(8,128)S(1)}, f32[2,2,128,256]{3,2,1,0:T(8,128)S(1)}, u32[]{:S(2)}, u32[]{:S(2)}) collective-permute-start(f32[2,2,128,256]{3,2,1,0:T(8,128)S(1)} %get-tuple-element.25), channel_id=1, source_target_pairs={{17,19},{19,21},{21,23},{23,25},{25,27},{27,29},{29,31},{18,16},{2... | collective-permute-start | bytes 1572872 | tf_op jit(solution)/shard_map/ppermute | solution.py:311
  22.2 15.1 %collective-permute-start.12 = (f32[2,2,128,256]{3,2,1,0:T(8,128)S(1)}, f32[2,2,128,256]{3,2,1,0:T(8,128)S(1)}, u32[]{:S(2)}, u32[]{:S(2)}) collective-permute-start(f32[2,2,128,256]{3,2,1,0:T(8,128)S(1)} %get-tuple-element.26), channel_id=1, source_target_pairs={{1,19},{3,21},{5,23},{7,25},{9,27},{11,29},{13,31},{2,16},{4,18},{... | collective-permute-start | bytes 1572872 | tf_op jit(solution)/shard_map/ppermute | solution.py:311
  24.7 27.6 %collective-permute-start.3 = (f32[2,2,128,256]{3,2,1,0:T(8,128)S(1)}, f32[2,2,128,256]{3,2,1,0:T(8,128)S(1)}, u32[]{:S(2)}, u32[]{:S(2)}) collective-permute-start(f32[2,2,128,256]{3,2,1,0:T(8,128)S(1)} %get-tuple-element.23), channel_id=1, source_target_pairs={{0,1},{1,0},{2,3},{3,2},{4,5},{5,4},{6,7},{7,6},{8,9},{9,8},{10,11... | collective-permute-start | bytes 1572872 | tf_op jit(solution)/shard_map/ppermute | solution.py:311
  28.6 25.0 %collective-permute-start.4 = (f32[2,2,128,256]{3,2,1,0:T(8,128)S(1)}, f32[2,2,128,256]{3,2,1,0:T(8,128)S(1)}, u32[]{:S(2)}, u32[]{:S(2)}) collective-permute-start(f32[2,2,128,256]{3,2,1,0:T(8,128)S(1)} %get-tuple-element.24), channel_id=1, source_target_pairs={{16,1},{17,0},{18,3},{19,2},{20,5},{21,4},{22,7},{23,6},{24,9},{25... | collective-permute-start | bytes 1572872 | tf_op jit(solution)/shard_map/ppermute | solution.py:311
  31.7 23.9 %collective-permute-start.5 = (f32[2,2,128,256]{3,2,1,0:T(8,128)S(1)}, f32[2,2,128,256]{3,2,1,0:T(8,128)S(1)}, u32[]{:S(2)}, u32[]{:S(2)}) collective-permute-start(f32[2,2,128,256]{3,2,1,0:T(8,128)S(1)} %get-tuple-element.25), channel_id=1, source_target_pairs={{1,3},{3,5},{5,7},{7,9},{9,11},{11,13},{13,15},{2,0},{4,2},{6,4},{... | collective-permute-start | bytes 1572872 | tf_op jit(solution)/shard_map/ppermute | solution.py:311
  32.4 24.5 %collective-permute-start.6 = (f32[2,2,128,256]{3,2,1,0:T(8,128)S(1)}, f32[2,2,128,256]{3,2,1,0:T(8,128)S(1)}, u32[]{:S(2)}, u32[]{:S(2)}) collective-permute-start(f32[2,2,128,256]{3,2,1,0:T(8,128)S(1)} %get-tuple-element.26), channel_id=1, source_target_pairs={{17,3},{19,5},{21,7},{23,9},{25,11},{27,13},{29,15},{18,0},{20,2},... | collective-permute-start | bytes 1572872 | tf_op jit(solution)/shard_map/ppermute | solution.py:311
  51.0 19.5 %collective-permute-start.20 = (f32[2,2,128,256]{3,2,1,0:T(8,128)S(1)}, f32[2,2,128,256]{3,2,1,0:T(8,128)S(1)}, u32[]{:S(2)}, u32[]{:S(2)}) collective-permute-start(f32[2,2,128,256]{3,2,1,0:T(8,128)S(1)} %get-tuple-element.35), channel_id=1, source_target_pairs={{19,1},{21,3},{23,5},{25,7},{27,9},{29,11},{31,13},{16,2},{18,4},{... | collective-permute-start | bytes 1572872 | tf_op jit(solution)/shard_map/ppermute | solution.py:311
  52.3 19.5 %collective-permute-start.16 = (f32[2,2,128,256]{3,2,1,0:T(8,128)S(1)}, f32[2,2,128,256]{3,2,1,0:T(8,128)S(1)}, u32[]{:S(2)}, u32[]{:S(2)}) collective-permute-start(f32[2,2,128,256]{3,2,1,0:T(8,128)S(1)} %get-tuple-element.35), channel_id=1, source_target_pairs={{16,0},{17,1},{18,2},{19,3},{20,4},{21,5},{22,6},{23,7},{24,8},{25... | collective-permute-start | bytes 1572872 | tf_op jit(solution)/shard_map/ppermute | solution.py:311
  53.7 9.9 %collective-permute-start.13 = (f32[2,2,128,256]{3,2,1,0:T(8,128)S(1)}, f32[2,2,128,256]{3,2,1,0:T(8,128)S(1)}, u32[]{:S(2)}, u32[]{:S(2)}) collective-permute-start(f32[2,2,128,256]{3,2,1,0:T(8,128)S(1)} %get-tuple-element.30), channel_id=1, source_target_pairs={{16,17},{17,16},{18,19},{19,18},{20,21},{21,20},{22,23},{23,22},{2... | collective-permute-start | bytes 1572872 | tf_op jit(solution)/shard_map/ppermute | solution.py:311
  55.6 12.9 %collective-permute-start.14 = (f32[2,2,128,256]{3,2,1,0:T(8,128)S(1)}, f32[2,2,128,256]{3,2,1,0:T(8,128)S(1)}, u32[]{:S(2)}, u32[]{:S(2)}) collective-permute-start(f32[2,2,128,256]{3,2,1,0:T(8,128)S(1)} %get-tuple-element.31), channel_id=1, source_target_pairs={{16,1},{17,0},{18,3},{19,2},{20,5},{21,4},{22,7},{23,6},{24,9},{25... | collective-permute-start | bytes 1572872 | tf_op jit(solution)/shard_map/ppermute | solution.py:311
  56.9 34.1 %copy-start.2 = (s32[2,2]{1,0:T(2,128)S(1)}, s32[2,2]{1,0:T(2,128)}, u32[]{:S(2)}) copy-start(s32[2,2]{1,0:T(2,128)} %own.1) | copy-start | bytes 52
  56.9 12.8 %collective-permute-start.19 = (f32[2,2,128,256]{3,2,1,0:T(8,128)S(1)}, f32[2,2,128,256]{3,2,1,0:T(8,128)S(1)}, u32[]{:S(2)}, u32[]{:S(2)}) collective-permute-start(f32[2,2,128,256]{3,2,1,0:T(8,128)S(1)} %get-tuple-element.34.refs_5_), channel_id=1, source_target_pairs={{19,17},{21,19},{23,21},{25,23},{27,25},{29,27},{31,29},{16,18},{1... | collective-permute-start | bytes 1572872 | tf_op jit(solution)/shard_map/ppermute | solution.py:311
  63.6 9.5 %collective-permute-start.8 = (f32[2,2,128,256]{3,2,1,0:T(8,128)S(1)}, f32[2,2,128,256]{3,2,1,0:T(8,128)S(1)}, u32[]{:S(2)}, u32[]{:S(2)}) collective-permute-start(f32[2,2,128,256]{3,2,1,0:T(8,128)S(1)} %get-tuple-element.29), channel_id=1, source_target_pairs={{0,1},{1,0},{2,3},{3,2},{4,5},{5,4},{6,7},{7,6},{8,9},{9,8},{10,11... | collective-permute-start | bytes 1572872 | tf_op jit(solution)/shard_map/ppermute | solution.py:311
  68.5 12.3 %collective-permute-start.15 = (f32[2,2,128,256]{3,2,1,0:T(8,128)S(1)}, f32[2,2,128,256]{3,2,1,0:T(8,128)S(1)}, u32[]{:S(2)}, u32[]{:S(2)}) collective-permute-start(f32[2,2,128,256]{3,2,1,0:T(8,128)S(1)} %get-tuple-element.32), channel_id=1, source_target_pairs={{0,17},{1,16},{2,19},{3,18},{4,21},{5,20},{6,23},{7,22},{8,25},{9,... | collective-permute-start | bytes 1572872 | tf_op jit(solution)/shard_map/ppermute | solution.py:311
  69.8 11.0 %collective-permute-start.18 = (f32[2,2,128,256]{3,2,1,0:T(8,128)S(1)}, f32[2,2,128,256]{3,2,1,0:T(8,128)S(1)}, u32[]{:S(2)}, u32[]{:S(2)}) collective-permute-start(f32[2,2,128,256]{3,2,1,0:T(8,128)S(1)} %get-tuple-element.33.refs_4_), channel_id=1, source_target_pairs={{3,1},{5,3},{7,5},{9,7},{11,9},{13,11},{15,13},{0,2},{2,4},{4,6},{... | collective-permute-start | bytes 1572872 | tf_op jit(solution)/shard_map/ppermute | solution.py:311
  70.5 20.5 %collective-permute-start.21 = (f32[2,2,128,256]{3,2,1,0:T(8,128)S(1)}, f32[2,2,128,256]{3,2,1,0:T(8,128)S(1)}, u32[]{:S(2)}, u32[]{:S(2)}) collective-permute-start(f32[2,2,128,256]{3,2,1,0:T(8,128)S(1)} %get-tuple-element.36), channel_id=1, source_target_pairs={{3,17},{5,19},{7,21},{9,23},{11,25},{13,27},{15,29},{0,18},{2,20},... | collective-permute-start | bytes 1572872 | tf_op jit(solution)/shard_map/ppermute | solution.py:311
  71.8 19.2 %collective-permute-start.17 = (f32[2,2,128,256]{3,2,1,0:T(8,128)S(1)}, f32[2,2,128,256]{3,2,1,0:T(8,128)S(1)}, u32[]{:S(2)}, u32[]{:S(2)}) collective-permute-start(f32[2,2,128,256]{3,2,1,0:T(8,128)S(1)} %get-tuple-element.36), channel_id=1, source_target_pairs={{0,16},{1,17},{2,18},{3,19},{4,20},{5,21},{6,22},{7,23},{8,24},{9,... | collective-permute-start | bytes 1572872 | tf_op jit(solution)/shard_map/ppermute | solution.py:311

commit v2 on v1

--- a/solution.py
+++ b/solution.py
@@ -146,36 +146,26 @@
 
 def work_kernel(core, offsets, probe, kernel, table, target, *refs):
     mids, fars, nears, refs = refs[0:2], refs[2:4], refs[4:6], refs[6:]
-    tops, lows, (patches, waves, cur, third, own, sems) = refs[0:2], refs[2:4], refs[4:]
+    tops, lows, (patches, waves, cur) = refs[0:2], refs[2:4], refs[4:]
     count = patches.shape[0]
-    layers, parts, rows, patch = third.shape[1:]
+    layers, parts, rows, patch = mids[0].shape
     groups = (core, 1 - core)
 
     @pl.when(lax.axis_index("depth") == core)
     def _():
         tile = lax.axis_index("tile")
-        copies = []
-        for i, group in enumerate(groups):
-            part = patches.at[pl.ds(group * layers, layers), :, pl.ds(rows, rows), :]
-            copies += [
-                pltpu.make_async_copy(mids[i], part, sems.at[i, 0]),
-                pltpu.make_async_copy(fars[i], third.at[group], sems.at[i, 1]),
-                pltpu.make_async_copy(nears[i], own.at[group], sems.at[i, 2]),
-            ]
-        for copy in copies:
-            copy.start()
         down = top_row(offsets, core, tile ^ 1, rows)
         right = offsets[core, 1] % patch
         for c in range(2):
             waves[0, c] = pltpu.roll(pltpu.roll(probe[c], down, 0), right, 1)
         row = lax.broadcasted_iota(jnp.int32, (rows, patch), 0)
         from_own = (row < down) == (tile % 2 == 1)
-        for copy in copies:
-            copy.wait()
-        for s in range(count):
-            for c in range(parts):
-                g, r = divmod(s, layers)
-                patches[s, c, :rows] = jnp.where(from_own, own[g, r, c], third[g, r, c])
+        for i, group in enumerate(groups):
+            for r in range(layers):
+                for c in range(parts):
+                    s = group * layers + r
+                    patches[s, c, :rows] = jnp.where(from_own, nears[i][r, c], fars[i][r, c])
+                    patches[s, c, rows:] = mids[i][r, c]
         cur[0], cur[1] = times(patches.at[0], waves[0, 0], waves[0, 1], False)
 
         def step(s, unused):
@@ -183,7 +173,7 @@
             exit_step = s == count - 1
             residue = 2.0 * (a * a + b * b - target[...])
             kr = jnp.where(exit_step, residue, kernel[0])
-            ki = jnp.where(exit_step, 0.0, jnp.where(s < count, kernel[1], -kernel[1]))
+            ki = kernel[1] * jnp.where(exit_step, 0.0, jnp.where(s < count, 1.0, -1.0))
             a, b = kr * a - ki * b, kr * b + ki * a
             cur[0], cur[1] = inverse(a, b, table)
 
@@ -212,50 +202,26 @@
 
 
 def work(core, offsets, probe, kernel, table, target, *sources):
-    layers, parts, rows, patch = sources[0].shape
+    layers, parts, _, patch = sources[0].shape
     band = jax.ShapeDtypeStruct(sources[0].shape, F32)
     full_v = pltpu.VMEM((2 * layers, parts, patch, patch), F32)
-    band_v = pltpu.VMEM((2, layers, parts, rows, patch), F32)
     flops = 28 * layers * 12 * patch**3
     return pl.pallas_call(
         functools.partial(work_kernel, core),
         out_shape=[band] * 4,
-        in_specs=[SMEM] + [VMEM] * 4 + [ANY] * 6,
+        in_specs=[SMEM] + [VMEM] * 10,
         out_specs=[VMEM] * 4,
-        scratch_shapes=[
-            full_v,
-            full_v,
-            pltpu.VMEM((parts, patch, patch), F32),
-            band_v,
-            band_v,
-            pltpu.SemaphoreType.DMA((2, 3)),
-        ],
+        scratch_shapes=[full_v, full_v, pltpu.VMEM((parts, patch, patch), F32)],
         cost_estimate=pl.CostEstimate(flops=flops, bytes_accessed=8 << 20, transcendentals=0),
         compiler_params=limit(28),
         name="work",
     )(offsets, probe, kernel, table, target, *sources)
 
 
-def pick(depth, at_zero, at_one, dst, sem):
-    @pl.when(depth == 0)
-    def _():
-        pltpu.make_async_copy(at_zero, dst, sem).start()
-
-    @pl.when(depth != 0)
-    def _():
-        pltpu.make_async_copy(at_one, dst, sem).start()
-
-    return pltpu.make_async_copy(at_zero, dst, sem)
-
-
 def gather_kernel(own, partner, their, *refs):
-    sources, (out, windows, total, sems, out_sems) = refs[:12], refs[12:]
-    layers, parts, rows, patch = windows.shape[1:]
+    sources, (out, total, out_sems) = refs[:12], refs[12:]
+    layers, parts, rows, patch = sources[0].shape
     depth, tile = lax.axis_index("depth"), lax.axis_index("tile")
-    copies = [
-        pick(depth, sources[2 * i], sources[2 * i + 1], windows.at[i], sems.at[i])
-        for i in range(6)
-    ]
     row = lax.broadcasted_iota(jnp.int32, (rows, patch), 0)
     lane = lax.broadcasted_iota(jnp.int32, (rows, patch), 1)
     odd = tile % 2 == 1
@@ -267,14 +233,12 @@
         holder = (tile, tile ^ 1, jnp.where(odd, tile + 1, tile - 1))[i // 2]
         start, shift = place(offsets[position, 1], patch, total.shape[3])
         facts.append((start, shift, top_row(offsets, position, holder, rows)))
-    for copy in copies:
-        copy.wait()
     sends = []
     for s in range(layers):
         for c in range(parts):
             for i in range(6):
                 start, shift, down = facts[i]
-                value = windows[i, s, c]
+                value = jnp.where(depth == 0, sources[2 * i][s, c], sources[2 * i + 1][s, c])
                 if i >= 2:
                     above = row < down
                     keep = (above == odd) if i < 4 else (above != odd)
@@ -325,11 +289,10 @@
         x = jnp.dot(pick_one, x, precision=lax.Precision.HIGHEST)
         return jnp.dot(x, pick_one.T, precision=lax.Precision.HIGHEST)
 
-    phase = reorder(fresnel_phase)
-    kernel = jnp.stack([jnp.cos(phase), jnp.sin(phase)], 0)
-    their, kernel = lax.optimization_barrier((their, kernel))
-    found = extract(specimen, [their, scan_offsets, partner], patch)
-    far, mid, near = found[0:2], found[2:4], found[4:6]
+    offsets = pltpu.with_memory_space_constraint(scan_offsets, pltpu.HBM)
+    found = extract(specimen, [their, offsets], patch)
+    far, mid = found[0:2], found[2:4]
+    near = extract(specimen, [partner], patch)
     mids, fars = [], []
     for core in range(2):
         for step in range(2):
@@ -337,6 +300,8 @@
             mids.append(send(mid[step], swap, hop))
             fars.append(send(far[step], outward, hop))
     near_other = send(near[1], stay, cross)
+    phase = reorder(fresnel_phase)
+    kernel = jnp.stack([jnp.cos(phase), jnp.sin(phase)], 0)
     target = reorder(target)
 
     kept, others, lows, tops = [], [], [], []
@@ -358,14 +323,9 @@
     return pl.pallas_call(
         gather_kernel,
         out_shape=jax.ShapeDtypeStruct(specimen.shape, F32),
-        in_specs=[SMEM] * 3 + [ANY] * 12,
+        in_specs=[SMEM] * 3 + [VMEM] * 12,
         out_specs=ANY,
-        scratch_shapes=[
-            pltpu.VMEM((6, layers, parts, rows, patch), F32),
-            pltpu.VMEM(specimen.shape, F32),
-            pltpu.SemaphoreType.DMA((6,)),
-            pltpu.SemaphoreType.DMA((layers, parts)),
-        ],
+        scratch_shapes=[pltpu.VMEM(specimen.shape, F32), pltpu.SemaphoreType.DMA((layers, parts))],
         cost_estimate=pl.CostEstimate(flops=6 << 20, bytes_accessed=7 << 20, transcendentals=0),
         compiler_params=limit(16),
         name="gather",

time: 94.9 us -> 95.1 us (level)
    pallas_call x1 -> x2, Pallas kernels: 3.73 us -> 5.19 us  [extract(): pl.pallas_call(functools.partial(extract_kernel, count), out_shape=[jax.S...]
  transfers between devices with their start and end apart: 22 -> 22, of which waited for: 5 -> 5; matrix products, arithmetic and copies ran while one was open for 5% -> 5% of each run, Pallas kernels for 19% -> 20%
where the time goes in v2:
time: 95.1 us; the launch traced here: 94.6 us
  starting transfers between devices  37.7 us (40%)
  waiting for transfers between devices  29 us (30%)
  Pallas kernels  22.2 us (23%)
  matrix products  5.12 us (5%)
    ppermute x22, starting transfers between devices, send(): lax.ppermute(value, AXES, [(a * tiles + s, b * tiles + t) for a, b in hop...  37.7 us
    ppermute x22, waiting for transfers between devices, send(): lax.ppermute(value, AXES, [(a * tiles + s, b * tiles + t) for a, b in hop...  29 us
    pallas_call x2, Pallas kernels, work(): pl.pallas_call(functools.partial(work_kernel, core), out_shape=[band] * 4...  13.8 us
    pallas_call x2, Pallas kernels, extract(): pl.pallas_call(functools.partial(extract_kernel, count), out_shape=[jax.S...  5.19 us
    pallas_call x1, Pallas kernels, local(): pl.pallas_call(gather_kernel, out_shape=jax.ShapeDtypeStruct(specimen.sha...  3.21 us
    dot_general x2, matrix products, reorder(): return jnp.dot(x, pick_one.T, precision=lax.Precision.HIGHEST)  3.12 us
    dot_general x2, matrix products, reorder(): x = jnp.dot(pick_one, x, precision=lax.Precision.HIGHEST)  2 us
  transfers between devices with their start and end apart: 22, of which 5 were waited for; matrix products, arithmetic and copies ran while one was open for 5% of the time, Pallas kernels for 20%

profile of v2, /device:TPU:25, one launch (start us, length us, event | category | flops | bytes accessed | tf_op | source)
XLA Modules:
  0.0 94.6 jit_solution(10553680766294552268)
XLA Ops:
  0.0 4.1 %collective-permute-start.1 = (s32[2,2]{1,0:T(2,128)}, s32[2,2]{1,0:T(2,128)S(1)}, u32[]{:S(2)}, u32[]{:S(2)}) collective-permute-start(s32[2,2]{1,0:T(2,128)} %own.1), channel_id=1, source_target_pairs={{1,2},{3,4},{5,6},{7,8},{9,10},{11,12},{13,14},{2,1},{4,3},{6,5},{... | collective-permute-start | bytes 56 | tf_op jit(solution)/shard_map/ppermute | solution.py:275
  4.1 0.4 collective-permute-start
  4.6 1.2 %collective-permute-start.2 = (f32[256,256]{1,0:T(8,128)S(1)}, f32[256,256]{1,0:T(8,128)S(1)}, u32[]{:S(2)}, u32[]{:S(2)}) collective-permute-start(f32[256,256]{1,0:T(8,128)S(1)} %dynamic-slice_bitcast_fusion), channel_id=1, source_target_pairs={{0,1},{1,0},{2,3},{3,2},{4,5},{5,4},{6,7},{7,6},{8,9},{9,8},{10,11... | collective-permute-start | bytes 786440 | tf_op jit(solution)/shard_map/ppermute | solution.py:275
  5.7 1.4 %fusion = f32[256,256]{1,0:T(8,128)S(1)} fusion(f32[256,256]{1,0:T(8,128)} %constant.17.clone, f32[256,256]{1,0:T(8,128)} %param.10), kind=kOutput, calls=%fused_computation.4 | convolution fusion | flops 201326592 | bytes 786432 | tf_op jit(solution)/shard_map/dot_general | solution.py:289
  7.1 2.5 %cosine_bitcast_fusion = (f32[1,256,256]{2,1,0:T(8,128)S(1)}, f32[1,256,256]{2,1,0:T(8,128)S(1)}) fusion(f32[256,256]{1,0:T(8,128)S(1)} %fusion, f32[256,256]{1,0:T(8,128)} %constant.17.clone), kind=kOutput, calls=%fused_computation.3 | convolution fusion | flops 201326592 | bytes 1048576 | tf_op jit(solution)/shard_map/dot_general | solution.py:290
  9.7 0.0 copy-start.4
  9.7 0.0 collective-permute-done.refs_0_.offsets.partner
  9.7 2.2 %extract.3 = (f32[2,2,128,256]{3,2,1,0:T(8,128)S(1)}, f32[2,2,128,256]{3,2,1,0:T(8,128)S(1)}) custom-call(s32[2,2]{1,0:T(2,128)S(1)} %collective-permute-done.refs_0_.offsets.partner, f32[2,2,128,2048]{3,2,1,0:T(8,128)} %refs_1_.3), custom_call_target="tpu_custom_call" | custom-call | flops 262144 | bytes 3145728 | tf_op jit(solution)/shard_map/extract/pallas_call | solution.py:128
  11.8 0.0 copy-start.2
  11.9 0.0 copy-start.3
  11.9 1.6 %collective-permute-start.7 = (f32[2,2,128,256]{3,2,1,0:T(8,128)S(1)}, f32[2,2,128,256]{3,2,1,0:T(8,128)S(1)}, u32[]{:S(2)}, u32[]{:S(2)}) collective-permute-start(f32[2,2,128,256]{3,2,1,0:T(8,128)S(1)} %get-tuple-element.24), channel_id=1, source_target_pairs={{0,16},{1,17},{2,18},{3,19},{4,20},{5,21},{6,22},{7,23},{8,24},{9,... | collective-permute-start | bytes 1572872 | tf_op jit(solution)/shard_map/ppermute | solution.py:275
  13.5 3.0 %extract.2 = (f32[2,2,128,256]{3,2,1,0:T(8,128)S(1)}, f32[2,2,128,256]{3,2,1,0:T(8,128)S(1)}, f32[2,2,128,256]{3,2,1,0:T(8,128)S(1)}, f32[2,2,128,256]{3,2,1,0:T(8,128)S(1)}) custom-call(s32[2,2]{1,0:T(2,128)S(1)} %collective-permute-done.1.refs_0_.their, s32[2,2]{1,0:T(2,128)} %own.1, f32[2,2,128,2048]{3,2,1,0:T(8,128)} %refs_1_.3), custom_call_target="tpu_custom_call" | custom-call | flops 524288 | bytes 6291456 | tf_op jit(solution)/shard_map/extract/pallas_call | solution.py:128
  16.5 2.2 %collective-permute-start.9 = (f32[2,2,128,256]{3,2,1,0:T(8,128)S(1)}, f32[2,2,128,256]{3,2,1,0:T(8,128)S(1)}, u32[]{:S(2)}, u32[]{:S(2)}) collective-permute-start(f32[2,2,128,256]{3,2,1,0:T(8,128)S(1)} %get-tuple-element.19), channel_id=1, source_target_pairs={{16,17},{17,16},{18,19},{19,18},{20,21},{21,20},{22,23},{23,22},{2... | collective-permute-start | bytes 1572872 | tf_op jit(solution)/shard_map/ppermute | solution.py:275
  18.7 1.3 %collective-permute-start.10 = (f32[2,2,128,256]{3,2,1,0:T(8,128)S(1)}, f32[2,2,128,256]{3,2,1,0:T(8,128)S(1)}, u32[]{:S(2)}, u32[]{:S(2)}) collective-permute-start(f32[2,2,128,256]{3,2,1,0:T(8,128)S(1)} %get-tuple-element.20), channel_id=1, source_target_pairs={{0,17},{1,16},{2,19},{3,18},{4,21},{5,20},{6,23},{7,22},{8,25},{9,... | collective-permute-start | bytes 1572872 | tf_op jit(solution)/shard_map/ppermute | solution.py:275
  20.0 3.1 %collective-permute-start.11 = (f32[2,2,128,256]{3,2,1,0:T(8,128)S(1)}, f32[2,2,128,256]{3,2,1,0:T(8,128)S(1)}, u32[]{:S(2)}, u32[]{:S(2)}) collective-permute-start(f32[2,2,128,256]{3,2,1,0:T(8,128)S(1)} %get-tuple-element.21), channel_id=1, source_target_pairs={{17,19},{19,21},{21,23},{23,25},{25,27},{27,29},{29,31},{18,16},{2... | collective-permute-start | bytes 1572872 | tf_op jit(solution)/shard_map/ppermute | solution.py:275
  23.1 0.0 collective-permute-done.2
  23.1 1.3 %collective-permute-start.12 = (f32[2,2,128,256]{3,2,1,0:T(8,128)S(1)}, f32[2,2,128,256]{3,2,1,0:T(8,128)S(1)}, u32[]{:S(2)}, u32[]{:S(2)}) collective-permute-start(f32[2,2,128,256]{3,2,1,0:T(8,128)S(1)} %get-tuple-element.22), channel_id=1, source_target_pairs={{1,19},{3,21},{5,23},{7,25},{9,27},{11,29},{13,31},{2,16},{4,18},{... | collective-permute-start | bytes 1572872 | tf_op jit(solution)/shard_map/ppermute | solution.py:275
  24.5 0.6 fusion.1
  25.1 0.6 fusion.2.target
  25.7 0.0 collective-permute-done.7.refs_5_
  25.7 0.7 collective-permute-start.3
  26.4 2.8 %collective-permute-done.9.refs_0_ = f32[2,2,128,256]{3,2,1,0:T(8,128)S(1)} collective-permute-done((f32[2,2,128,256]{3,2,1,0:T(8,128)S(1)}, f32[2,2,128,256]{3,2,1,0:T(8,128)S(1)}, u32[]{:S(2)}, u32[]{:S(2)}) %collective-permute-start.9) | collective-permute-done | bytes 524320 | tf_op jit(solution)/shard_map/ppermute | solution.py:275
  29.2 3.4 %collective-permute-start.4 = (f32[2,2,128,256]{3,2,1,0:T(8,128)S(1)}, f32[2,2,128,256]{3,2,1,0:T(8,128)S(1)}, u32[]{:S(2)}, u32[]{:S(2)}) collective-permute-start(f32[2,2,128,256]{3,2,1,0:T(8,128)S(1)} %get-tuple-element.20), channel_id=1, source_target_pairs={{16,1},{17,0},{18,3},{19,2},{20,5},{21,4},{22,7},{23,6},{24,9},{25... | collective-permute-start | bytes 1572872 | tf_op jit(solution)/shard_map/ppermute | solution.py:275
  32.6 0.0 collective-permute-done.10.refs_1_
  32.6 0.7 collective-permute-start.5
  33.3 4.8 %collective-permute-start.6 = (f32[2,2,128,256]{3,2,1,0:T(8,128)S(1)}, f32[2,2,128,256]{3,2,1,0:T(8,128)S(1)}, u32[]{:S(2)}, u32[]{:S(2)}) collective-permute-start(f32[2,2,128,256]{3,2,1,0:T(8,128)S(1)} %get-tuple-element.22), channel_id=1, source_target_pairs={{17,3},{19,5},{21,7},{23,9},{25,11},{27,13},{29,15},{18,0},{20,2},... | collective-permute-start | bytes 1572872 | tf_op jit(solution)/shard_map/ppermute | solution.py:275
  38.1 13.3 %work.3 = (f32[2,2,128,256]{3,2,1,0:T(8,128)S(1)}, f32[2,2,128,256]{3,2,1,0:T(8,128)S(1)}, f32[2,2,128,256]{3,2,1,0:T(8,128)S(1)}, f32[2,2,128,256]{3,2,1,0:T(8,128)S(1)}) custom-call(s32[2,2]{1,0:T(2,128)S(1)} %collective-permute-done.refs_0_.offsets.partner, f32[2,256,256]{2,1,0:T(8,128)S(1)} %copy-done.2, f32[2,256,256]{2,1,0:T(8,128)S(1)} %pad_maximum_fusion.kernel, ...), custom_call_target="tpu_custom_call" | custom-call | flops 11274289152 | bytes 8388608 | tf_op jit(solution)/shard_map/work/pallas_call | solution.py:209
  51.4 1.3 %collective-permute-start.20 = (f32[2,2,128,256]{3,2,1,0:T(8,128)S(1)}, f32[2,2,128,256]{3,2,1,0:T(8,128)S(1)}, u32[]{:S(2)}, u32[]{:S(2)}) collective-permute-start(f32[2,2,128,256]{3,2,1,0:T(8,128)S(1)} %get-tuple-element.31), channel_id=1, source_target_pairs={{19,1},{21,3},{23,5},{25,7},{27,9},{29,11},{31,13},{16,2},{18,4},{... | collective-permute-start | bytes 1572872 | tf_op jit(solution)/shard_map/ppermute | solution.py:275
  52.8 1.3 %collective-permute-start.16 = (f32[2,2,128,256]{3,2,1,0:T(8,128)S(1)}, f32[2,2,128,256]{3,2,1,0:T(8,128)S(1)}, u32[]{:S(2)}, u32[]{:S(2)}) collective-permute-start(f32[2,2,128,256]{3,2,1,0:T(8,128)S(1)} %get-tuple-element.31), channel_id=1, source_target_pairs={{16,0},{17,1},{18,2},{19,3},{20,4},{21,5},{22,6},{23,7},{24,8},{25... | collective-permute-start | bytes 1572872 | tf_op jit(solution)/shard_map/ppermute | solution.py:275
  54.1 0.0 collective-permute-done.4.refs_1_
  54.1 1.9 %collective-permute-start.13 = (f32[2,2,128,256]{3,2,1,0:T(8,128)S(1)}, f32[2,2,128,256]{3,2,1,0:T(8,128)S(1)}, u32[]{:S(2)}, u32[]{:S(2)}) collective-permute-start(f32[2,2,128,256]{3,2,1,0:T(8,128)S(1)} %get-tuple-element.26), channel_id=1, source_target_pairs={{16,17},{17,16},{18,19},{19,18},{20,21},{21,20},{22,23},{23,22},{2... | collective-permute-start | bytes 1572872 | tf_op jit(solution)/shard_map/ppermute | solution.py:275
  56.0 1.3 %collective-permute-start.14 = (f32[2,2,128,256]{3,2,1,0:T(8,128)S(1)}, f32[2,2,128,256]{3,2,1,0:T(8,128)S(1)}, u32[]{:S(2)}, u32[]{:S(2)}) collective-permute-start(f32[2,2,128,256]{3,2,1,0:T(8,128)S(1)} %get-tuple-element.27), channel_id=1, source_target_pairs={{16,1},{17,0},{18,3},{19,2},{20,5},{21,4},{22,7},{23,6},{24,9},{25... | collective-permute-start | bytes 1572872 | tf_op jit(solution)/shard_map/ppermute | solution.py:275
  57.4 0.0 collective-permute-done.6.refs_3_
  57.4 0.0 copy-start.1
  57.4 1.9 %collective-permute-start.19 = (f32[2,2,128,256]{3,2,1,0:T(8,128)S(1)}, f32[2,2,128,256]{3,2,1,0:T(8,128)S(1)}, u32[]{:S(2)}, u32[]{:S(2)}) collective-permute-start(f32[2,2,128,256]{3,2,1,0:T(8,128)S(1)} %get-tuple-element.30.refs_5_), channel_id=1, source_target_pairs={{19,17},{21,19},{23,21},{25,23},{27,25},{29,27},{31,29},{16,18},{1... | collective-permute-start | bytes 1572872 | tf_op jit(solution)/shard_map/ppermute | solution.py:275
  59.3 0.6 work.2
  59.9 4.1 %collective-permute-done.13.refs_1_ = f32[2,2,128,256]{3,2,1,0:T(8,128)S(1)} collective-permute-done((f32[2,2,128,256]{3,2,1,0:T(8,128)S(1)}, f32[2,2,128,256]{3,2,1,0:T(8,128)S(1)}, u32[]{:S(2)}, u32[]{:S(2)}) %collective-permute-start.13) | collective-permute-done | bytes 524320 | tf_op jit(solution)/shard_map/ppermute | solution.py:275
  64.0 0.7 collective-permute-start.8
  64.7 4.1 %collective-permute-done.14.refs_2_ = f32[2,2,128,256]{3,2,1,0:T(8,128)S(1)} collective-permute-done((f32[2,2,128,256]{3,2,1,0:T(8,128)S(1)}, f32[2,2,128,256]{3,2,1,0:T(8,128)S(1)}, u32[]{:S(2)}, u32[]{:S(2)}) %collective-permute-start.14) | collective-permute-done | bytes 524320 | tf_op jit(solution)/shard_map/ppermute | solution.py:275
  68.8 1.3 %collective-permute-start.15 = (f32[2,2,128,256]{3,2,1,0:T(8,128)S(1)}, f32[2,2,128,256]{3,2,1,0:T(8,128)S(1)}, u32[]{:S(2)}, u32[]{:S(2)}) collective-permute-start(f32[2,2,128,256]{3,2,1,0:T(8,128)S(1)} %get-tuple-element.28), channel_id=1, source_target_pairs={{0,17},{1,16},{2,19},{3,18},{4,21},{5,20},{6,23},{7,22},{8,25},{9,... | collective-permute-start | bytes 1572872 | tf_op jit(solution)/shard_map/ppermute | solution.py:275
  70.1 0.0 collective-permute-done.19.refs_9_
  70.1 0.7 collective-permute-start.18
  70.8 0.0 collective-permute-done.20.refs_10_
  70.8 1.3 %collective-permute-start.21 = (f32[2,2,128,256]{3,2,1,0:T(8,128)S(1)}, f32[2,2,128,256]{3,2,1,0:T(8,128)S(1)}, u32[]{:S(2)}, u32[]{:S(2)}) collective-permute-start(f32[2,2,128,256]{3,2,1,0:T(8,128)S(1)} %get-tuple-element.32), channel_id=1, source_target_pairs={{3,17},{5,19},{7,21},{9,23},{11,25},{13,27},{15,29},{0,18},{2,20},... | collective-permute-start | bytes 1572872 | tf_op jit(solution)/shard_map/ppermute | solution.py:275
  72.2 1.3 %collective-permute-start.17 = (f32[2,2,128,256]{3,2,1,0:T(8,128)S(1)}, f32[2,2,128,256]{3,2,1,0:T(8,128)S(1)}, u32[]{:S(2)}, u32[]{:S(2)}) collective-permute-start(f32[2,2,128,256]{3,2,1,0:T(8,128)S(1)} %get-tuple-element.32), channel_id=1, source_target_pairs={{0,16},{1,17},{2,18},{3,19},{4,20},{5,21},{6,22},{7,23},{8,24},{9,... | collective-permute-start | bytes 1572872 | tf_op jit(solution)/shard_map/ppermute | solution.py:275
  73.5 7.7 %collective-permute-done.15.refs_3_ = f32[2,2,128,256]{3,2,1,0:T(8,128)S(1)} collective-permute-done((f32[2,2,128,256]{3,2,1,0:T(8,128)S(1)}, f32[2,2,128,256]{3,2,1,0:T(8,128)S(1)}, u32[]{:S(2)}, u32[]{:S(2)}) %collective-permute-start.15) | collective-permute-done | bytes 524320 | tf_op jit(solution)/shard_map/ppermute | solution.py:275
  81.2 10.2 %collective-permute-done.21.refs_11_ = f32[2,2,128,256]{3,2,1,0:T(8,128)S(1)} collective-permute-done((f32[2,2,128,256]{3,2,1,0:T(8,128)S(1)}, f32[2,2,128,256]{3,2,1,0:T(8,128)S(1)}, u32[]{:S(2)}, u32[]{:S(2)}) %collective-permute-start.21) | collective-permute-done | bytes 524320 | tf_op jit(solution)/shard_map/ppermute | solution.py:275
  91.4 3.2 %gather.1 = f32[2,2,128,2048]{3,2,1,0:T(8,128)} custom-call(s32[2,2]{1,0:T(2,128)S(1)} %copy-done.1, s32[2,2]{1,0:T(2,128)S(1)} %collective-permute-done.refs_0_.offsets.partner, s32[2,2]{1,0:T(2,128)S(1)} %collective-permute-done.1.refs_0_.their, f32[2,2,128,256]{3,2,1,0:T(8,128)S(1)} %collective-permute-done.8.refs_0_, ...), custom_call_target="tpu_custom_call" | custom-call | flops 6291456 | bytes 7340032 | tf_op jit(solution)/shard_map/gather/pallas_call | solution.py:323
  (17 shorter events, 0.1 us)
Async XLA Ops:
  0.0 4.5 %copy-start = (f32[2,256,256]{2,1,0:T(8,128)S(1)}, f32[2,256,256]{2,1,0:T(8,128)}, u32[]{:S(2)}) copy-start(f32[2,256,256]{2,1,0:T(8,128)} %param.11) | copy-start | bytes 1572868
  0.0 13.4 %collective-permute-start.1 = (s32[2,2]{1,0:T(2,128)}, s32[2,2]{1,0:T(2,128)S(1)}, u32[]{:S(2)}, u32[]{:S(2)}) collective-permute-start(s32[2,2]{1,0:T(2,128)} %own.1), channel_id=1, source_target_pairs={{1,2},{3,4},{5,6},{7,8},{9,10},{11,12},{13,14},{2,1},{4,3},{6,5},{... | collective-permute-start | bytes 56 | tf_op jit(solution)/shard_map/ppermute | solution.py:275
  4.1 5.6 %collective-permute-start = (s32[2,2]{1,0:T(2,128)}, s32[2,2]{1,0:T(2,128)S(1)}, u32[]{:S(2)}, u32[]{:S(2)}) collective-permute-start(s32[2,2]{1,0:T(2,128)} %own.1), channel_id=1, source_target_pairs={{0,1},{1,0},{2,3},{3,2},{4,5},{5,4},{6,7},{7,6},{8,9},{9,8},{10,11... | collective-permute-start | bytes 56 | tf_op jit(solution)/shard_map/ppermute | solution.py:275
  4.6 18.6 %collective-permute-start.2 = (f32[256,256]{1,0:T(8,128)S(1)}, f32[256,256]{1,0:T(8,128)S(1)}, u32[]{:S(2)}, u32[]{:S(2)}) collective-permute-start(f32[256,256]{1,0:T(8,128)S(1)} %dynamic-slice_bitcast_fusion), channel_id=1, source_target_pairs={{0,1},{1,0},{2,3},{3,2},{4,5},{5,4},{6,7},{7,6},{8,9},{9,8},{10,11... | collective-permute-start | bytes 786440 | tf_op jit(solution)/shard_map/ppermute | solution.py:275
  9.7 14.8 %copy-start.4 = (f32[256,256]{1,0:T(8,128)S(1)}, f32[256,256]{1,0:T(8,128)}, u32[]{:S(2)}) copy-start(f32[256,256]{1,0:T(8,128)} %constant.17.clone) | copy-start | bytes 786436
  11.8 26.3 %copy-start.2 = (f32[2,256,256]{2,1,0:T(8,128)S(1)}, f32[2,256,256]{2,1,0:T(8,128)}, u32[]{:S(2)}) copy-start(f32[2,256,256]{2,1,0:T(8,128)} %probe.3) | copy-start | bytes 1572868
  11.9 26.3 %copy-start.3 = (bf16[4,2,256,256]{3,2,1,0:T(8,128)(2,1)S(1)}, bf16[4,2,256,256]{3,2,1,0:T(8,128)(2,1)}, u32[]{:S(2)}) copy-start(bf16[4,2,256,256]{3,2,1,0:T(8,128)(2,1)} %constant.16.clone.table) | copy-start | bytes 3145732
  11.9 13.8 %collective-permute-start.7 = (f32[2,2,128,256]{3,2,1,0:T(8,128)S(1)}, f32[2,2,128,256]{3,2,1,0:T(8,128)S(1)}, u32[]{:S(2)}, u32[]{:S(2)}) collective-permute-start(f32[2,2,128,256]{3,2,1,0:T(8,128)S(1)} %get-tuple-element.24), channel_id=1, source_target_pairs={{0,16},{1,17},{2,18},{3,19},{4,20},{5,21},{6,22},{7,23},{8,24},{9,... | collective-permute-start | bytes 1572872 | tf_op jit(solution)/shard_map/ppermute | solution.py:275
  16.5 12.7 %collective-permute-start.9 = (f32[2,2,128,256]{3,2,1,0:T(8,128)S(1)}, f32[2,2,128,256]{3,2,1,0:T(8,128)S(1)}, u32[]{:S(2)}, u32[]{:S(2)}) collective-permute-start(f32[2,2,128,256]{3,2,1,0:T(8,128)S(1)} %get-tuple-element.19), channel_id=1, source_target_pairs={{16,17},{17,16},{18,19},{19,18},{20,21},{21,20},{22,23},{23,22},{2... | collective-permute-start | bytes 1572872 | tf_op jit(solution)/shard_map/ppermute | solution.py:275
  18.7 13.9 %collective-permute-start.10 = (f32[2,2,128,256]{3,2,1,0:T(8,128)S(1)}, f32[2,2,128,256]{3,2,1,0:T(8,128)S(1)}, u32[]{:S(2)}, u32[]{:S(2)}) collective-permute-start(f32[2,2,128,256]{3,2,1,0:T(8,128)S(1)} %get-tuple-element.20), channel_id=1, source_target_pairs={{0,17},{1,16},{2,19},{3,18},{4,21},{5,20},{6,23},{7,22},{8,25},{9,... | collective-permute-start | bytes 1572872 | tf_op jit(solution)/shard_map/ppermute | solution.py:275
  20.0 13.3 %collective-permute-start.11 = (f32[2,2,128,256]{3,2,1,0:T(8,128)S(1)}, f32[2,2,128,256]{3,2,1,0:T(8,128)S(1)}, u32[]{:S(2)}, u32[]{:S(2)}) collective-permute-start(f32[2,2,128,256]{3,2,1,0:T(8,128)S(1)} %get-tuple-element.21), channel_id=1, source_target_pairs={{17,19},{19,21},{21,23},{23,25},{25,27},{27,29},{29,31},{18,16},{2... | collective-permute-start | bytes 1572872 | tf_op jit(solution)/shard_map/ppermute | solution.py:275
  23.1 15.0 %collective-permute-start.12 = (f32[2,2,128,256]{3,2,1,0:T(8,128)S(1)}, f32[2,2,128,256]{3,2,1,0:T(8,128)S(1)}, u32[]{:S(2)}, u32[]{:S(2)}) collective-permute-start(f32[2,2,128,256]{3,2,1,0:T(8,128)S(1)} %get-tuple-element.22), channel_id=1, source_target_pairs={{1,19},{3,21},{5,23},{7,25},{9,27},{11,29},{13,31},{2,16},{4,18},{... | collective-permute-start | bytes 1572872 | tf_op jit(solution)/shard_map/ppermute | solution.py:275
  25.7 27.1 %collective-permute-start.3 = (f32[2,2,128,256]{3,2,1,0:T(8,128)S(1)}, f32[2,2,128,256]{3,2,1,0:T(8,128)S(1)}, u32[]{:S(2)}, u32[]{:S(2)}) collective-permute-start(f32[2,2,128,256]{3,2,1,0:T(8,128)S(1)} %get-tuple-element.19), channel_id=1, source_target_pairs={{0,1},{1,0},{2,3},{3,2},{4,5},{5,4},{6,7},{7,6},{8,9},{9,8},{10,11... | collective-permute-start | bytes 1572872 | tf_op jit(solution)/shard_map/ppermute | solution.py:275
  29.2 24.9 %collective-permute-start.4 = (f32[2,2,128,256]{3,2,1,0:T(8,128)S(1)}, f32[2,2,128,256]{3,2,1,0:T(8,128)S(1)}, u32[]{:S(2)}, u32[]{:S(2)}) collective-permute-start(f32[2,2,128,256]{3,2,1,0:T(8,128)S(1)} %get-tuple-element.20), channel_id=1, source_target_pairs={{16,1},{17,0},{18,3},{19,2},{20,5},{21,4},{22,7},{23,6},{24,9},{25... | collective-permute-start | bytes 1572872 | tf_op jit(solution)/shard_map/ppermute | solution.py:275
  32.6 23.4 %collective-permute-start.5 = (f32[2,2,128,256]{3,2,1,0:T(8,128)S(1)}, f32[2,2,128,256]{3,2,1,0:T(8,128)S(1)}, u32[]{:S(2)}, u32[]{:S(2)}) collective-permute-start(f32[2,2,128,256]{3,2,1,0:T(8,128)S(1)} %get-tuple-element.21), channel_id=1, source_target_pairs={{1,3},{3,5},{5,7},{7,9},{9,11},{11,13},{13,15},{2,0},{4,2},{6,4},{... | collective-permute-start | bytes 1572872 | tf_op jit(solution)/shard_map/ppermute | solution.py:275
  33.3 24.0 %collective-permute-start.6 = (f32[2,2,128,256]{3,2,1,0:T(8,128)S(1)}, f32[2,2,128,256]{3,2,1,0:T(8,128)S(1)}, u32[]{:S(2)}, u32[]{:S(2)}) collective-permute-start(f32[2,2,128,256]{3,2,1,0:T(8,128)S(1)} %get-tuple-element.22), channel_id=1, source_target_pairs={{17,3},{19,5},{21,7},{23,9},{25,11},{27,13},{29,15},{18,0},{20,2},... | collective-permute-start | bytes 1572872 | tf_op jit(solution)/shard_map/ppermute | solution.py:275
  51.4 19.4 %collective-permute-start.20 = (f32[2,2,128,256]{3,2,1,0:T(8,128)S(1)}, f32[2,2,128,256]{3,2,1,0:T(8,128)S(1)}, u32[]{:S(2)}, u32[]{:S(2)}) collective-permute-start(f32[2,2,128,256]{3,2,1,0:T(8,128)S(1)} %get-tuple-element.31), channel_id=1, source_target_pairs={{19,1},{21,3},{23,5},{25,7},{27,9},{29,11},{31,13},{16,2},{18,4},{... | collective-permute-start | bytes 1572872 | tf_op jit(solution)/shard_map/ppermute | solution.py:275
  52.8 19.4 %collective-permute-start.16 = (f32[2,2,128,256]{3,2,1,0:T(8,128)S(1)}, f32[2,2,128,256]{3,2,1,0:T(8,128)S(1)}, u32[]{:S(2)}, u32[]{:S(2)}) collective-permute-start(f32[2,2,128,256]{3,2,1,0:T(8,128)S(1)} %get-tuple-element.31), channel_id=1, source_target_pairs={{16,0},{17,1},{18,2},{19,3},{20,4},{21,5},{22,6},{23,7},{24,8},{25... | collective-permute-start | bytes 1572872 | tf_op jit(solution)/shard_map/ppermute | solution.py:275
  54.1 9.9 %collective-permute-start.13 = (f32[2,2,128,256]{3,2,1,0:T(8,128)S(1)}, f32[2,2,128,256]{3,2,1,0:T(8,128)S(1)}, u32[]{:S(2)}, u32[]{:S(2)}) collective-permute-start(f32[2,2,128,256]{3,2,1,0:T(8,128)S(1)} %get-tuple-element.26), channel_id=1, source_target_pairs={{16,17},{17,16},{18,19},{19,18},{20,21},{21,20},{22,23},{23,22},{2... | collective-permute-start | bytes 1572872 | tf_op jit(solution)/shard_map/ppermute | solution.py:275
  56.0 12.8 %collective-permute-start.14 = (f32[2,2,128,256]{3,2,1,0:T(8,128)S(1)}, f32[2,2,128,256]{3,2,1,0:T(8,128)S(1)}, u32[]{:S(2)}, u32[]{:S(2)}) collective-permute-start(f32[2,2,128,256]{3,2,1,0:T(8,128)S(1)} %get-tuple-element.27), channel_id=1, source_target_pairs={{16,1},{17,0},{18,3},{19,2},{20,5},{21,4},{22,7},{23,6},{24,9},{25... | collective-permute-start | bytes 1572872 | tf_op jit(solution)/shard_map/ppermute | solution.py:275
  57.4 34.0 %copy-start.1 = (s32[2,2]{1,0:T(2,128)S(1)}, s32[2,2]{1,0:T(2,128)}, u32[]{:S(2)}) copy-start(s32[2,2]{1,0:T(2,128)} %own.1) | copy-start | bytes 52
  57.4 12.7 %collective-permute-start.19 = (f32[2,2,128,256]{3,2,1,0:T(8,128)S(1)}, f32[2,2,128,256]{3,2,1,0:T(8,128)S(1)}, u32[]{:S(2)}, u32[]{:S(2)}) collective-permute-start(f32[2,2,128,256]{3,2,1,0:T(8,128)S(1)} %get-tuple-element.30.refs_5_), channel_id=1, source_target_pairs={{19,17},{21,19},{23,21},{25,23},{27,25},{29,27},{31,29},{16,18},{1... | collective-permute-start | bytes 1572872 | tf_op jit(solution)/shard_map/ppermute | solution.py:275
  64.0 9.4 %collective-permute-start.8 = (f32[2,2,128,256]{3,2,1,0:T(8,128)S(1)}, f32[2,2,128,256]{3,2,1,0:T(8,128)S(1)}, u32[]{:S(2)}, u32[]{:S(2)}) collective-permute-start(f32[2,2,128,256]{3,2,1,0:T(8,128)S(1)} %get-tuple-element.25), channel_id=1, source_target_pairs={{0,1},{1,0},{2,3},{3,2},{4,5},{5,4},{6,7},{7,6},{8,9},{9,8},{10,11... | collective-permute-start | bytes 1572872 | tf_op jit(solution)/shard_map/ppermute | solution.py:275
  68.8 12.3 %collective-permute-start.15 = (f32[2,2,128,256]{3,2,1,0:T(8,128)S(1)}, f32[2,2,128,256]{3,2,1,0:T(8,128)S(1)}, u32[]{:S(2)}, u32[]{:S(2)}) collective-permute-start(f32[2,2,128,256]{3,2,1,0:T(8,128)S(1)} %get-tuple-element.28), channel_id=1, source_target_pairs={{0,17},{1,16},{2,19},{3,18},{4,21},{5,20},{6,23},{7,22},{8,25},{9,... | collective-permute-start | bytes 1572872 | tf_op jit(solution)/shard_map/ppermute | solution.py:275
  70.1 11.0 %collective-permute-start.18 = (f32[2,2,128,256]{3,2,1,0:T(8,128)S(1)}, f32[2,2,128,256]{3,2,1,0:T(8,128)S(1)}, u32[]{:S(2)}, u32[]{:S(2)}) collective-permute-start(f32[2,2,128,256]{3,2,1,0:T(8,128)S(1)} %get-tuple-element.29.refs_4_), channel_id=1, source_target_pairs={{3,1},{5,3},{7,5},{9,7},{11,9},{13,11},{15,13},{0,2},{2,4},{4,6},{... | collective-permute-start | bytes 1572872 | tf_op jit(solution)/shard_map/ppermute | solution.py:275
  70.8 20.5 %collective-permute-start.21 = (f32[2,2,128,256]{3,2,1,0:T(8,128)S(1)}, f32[2,2,128,256]{3,2,1,0:T(8,128)S(1)}, u32[]{:S(2)}, u32[]{:S(2)}) collective-permute-start(f32[2,2,128,256]{3,2,1,0:T(8,128)S(1)} %get-tuple-element.32), channel_id=1, source_target_pairs={{3,17},{5,19},{7,21},{9,23},{11,25},{13,27},{15,29},{0,18},{2,20},... | collective-permute-start | bytes 1572872 | tf_op jit(solution)/shard_map/ppermute | solution.py:275
  72.2 19.2 %collective-permute-start.17 = (f32[2,2,128,256]{3,2,1,0:T(8,128)S(1)}, f32[2,2,128,256]{3,2,1,0:T(8,128)S(1)}, u32[]{:S(2)}, u32[]{:S(2)}) collective-permute-start(f32[2,2,128,256]{3,2,1,0:T(8,128)S(1)} %get-tuple-element.32), channel_id=1, source_target_pairs={{0,16},{1,17},{2,18},{3,19},{4,20},{5,21},{6,22},{7,23},{8,24},{9,... | collective-permute-start | bytes 1572872 | tf_op jit(solution)/shard_map/ppermute | solution.py:275
